TPU v7x, 32 devices: a whole 2x2x4 slice. The times are simulated.
32 devices in a mesh: pipe: 2 (over x), dp: 4 (over y, core), tensor: 4 (over z).
Axes of the slice: x: 2, y: 2, z: 4, core: 2. Of those that a mesh axis runs over, the one named last changes fastest.
Arguments:
- inputs: bfloat16 [4, 1024, 1024], P(None, ('dp', 'tensor')), may hold values from -6 to 6
- segments: int32 [4, 1024], P(None, 'dp'), may hold values from 0 to 7, never falling along the last dimension, each value on 1 to 256 neighbouring positions
- cotangent: bfloat16 [4, 1024, 1024], P(None, ('dp', 'tensor')), may hold values from -6 to 6
- w_qkv: bfloat16 [2, 1024, 3, 1024], P('pipe', 'dp', None, 'tensor'), may hold values from -0.1875 to 0.1875
- w_o: bfloat16 [2, 1024, 1024], P('pipe', 'tensor', 'dp'), may hold values from -1.5 to 1.5
- w_in: bfloat16 [2, 1024, 4096], P('pipe', 'dp', 'tensor'), may hold values from -0.1875 to 0.1875
- w_out: bfloat16 [2, 4096, 1024], P('pipe', 'tensor', 'dp'), may hold values from -0.09375 to 0.09375
- ln_gains: float32 [2, 2, 1024], P('pipe'), may hold values from 0.1 to 1.9
- model_biases: float32 [2, 6, 1024], P('pipe'), may hold values from -1 to 1
- hidden_bias: float32 [2, 4096], P('pipe'), may hold values from -2.5 to 2.5
Outputs:
- section_outputs: bfloat16 [2, 4, 1024, 1024], P('pipe', None, ('dp', 'tensor'))
- input_grads: bfloat16 [2, 4, 1024, 1024], P('pipe', None, ('dp', 'tensor'))
- grad_qkv: float32 [2, 1024, 3, 1024], P('pipe', 'dp', None, 'tensor')
- grad_o: float32 [2, 1024, 1024], P('pipe', 'tensor', 'dp')
- grad_in: float32 [2, 1024, 4096], P('pipe', 'dp', 'tensor')
- grad_out: float32 [2, 4096, 1024], P('pipe', 'tensor', 'dp')
- grad_gains: float32 [2, 2, 1024], P('pipe', None, ('dp', 'tensor'))
- grad_biases: float32 [2, 6, 1024], P('pipe', None, ('dp', 'tensor'))
- grad_hidden_bias: float32 [2, 4096], P('pipe', ('dp', 'tensor'))
Inputs may be any that keep to these rules, and one draw needn't show every extreme that they name: `segments`: segment numbers never fall along a micro-batch's 1024 tokens; a segment holds 1 to 256 tokens and some segment holds exactly 256.
All inputs are finite; a program needn't handle non-finite values.
Results may differ from a plain program's by a relative error of at most 0.028.
Values may be sent and summed in bfloat16 or wider, within the bound.
No kernel may reach another device: no remote copies, remote signals or barrier semaphores. Data moves between devices by JAX's collectives and lax.ppermute only.
A program may use at most 128 MiB of HBM per device.

v0:
```python
import jax
import jax.numpy as jnp
from jax import lax
from jax.sharding import PartitionSpec as P

HEAD_DIM = 64


NORM_EPS = 1e-12
MASKED = -1000000000.0
ROOT_HALF = 0.7071067811865476
INV_ROOT_TWOPI = 0.3989422804014327


def shifted(block, axis, distance):
    devices = range(lax.axis_size(axis))
    route = [(i - distance, i) for i in devices if i - distance in devices]
    return lax.ppermute(block, axis, route)


def dot_rows(left_side, right_side):
    return lax.dot_general(
        left_side, right_side, (((0,), (0,)), ((), ())), preferred_element_type=jnp.float32
    )


def dot_cols(left_side, right_side):
    return lax.dot_general(
        left_side, right_side, (((1,), (1,)), ((), ())), preferred_element_type=jnp.float32
    )


def norm_forward(values, gain_row, shift_row):
    center = values - jnp.mean(values, axis=-1, keepdims=True)
    spread = jnp.mean(center * center, axis=-1, keepdims=True)
    inverse = lax.rsqrt(spread + NORM_EPS)
    scaled = center * inverse
    return (scaled * gain_row + shift_row, scaled, inverse)


def norm_backward(upstream, scaled, inverse, gain_row):
    weighted = upstream * gain_row
    inner_term = (
        weighted
        - jnp.mean(weighted, axis=-1, keepdims=True)
        - scaled * jnp.mean(weighted * scaled, axis=-1, keepdims=True)
    )
    return (inverse * inner_term, jnp.sum(upstream * scaled, axis=0), jnp.sum(upstream, axis=0))


def gelu_slope(values):
    return 0.5 * (1.0 + lax.erf(values * ROOT_HALF)) + values * INV_ROOT_TWOPI * jnp.exp(
        -0.5 * values * values
    )


def masked_scores(query_seq, key_seq, label_seq):
    scores = jnp.einsum(
        "qhe,khe->hqk", query_seq, key_seq, preferred_element_type=jnp.float32
    ) * HEAD_DIM ** (-0.5)
    allowed = label_seq[:, None] == label_seq[None, :]
    return jnp.where(allowed[None], scores, MASKED)


def attend(queries, key_rows, value_rows, labels):
    row_count, local_width = queries.shape
    heads_here = local_width // HEAD_DIM
    shaped = [
        member.reshape(1, row_count, heads_here, HEAD_DIM)
        for member in (queries, key_rows, value_rows)
    ]

    def one_sequence(pieces):
        query_seq, key_seq, value_seq, label_seq = pieces
        scores = masked_scores(query_seq, key_seq, label_seq)
        largest = jnp.max(scores, axis=-1, keepdims=True)
        total_mass = jnp.sum(jnp.exp(scores - largest), axis=-1, keepdims=True)
        log_total = largest + jnp.log(total_mass)
        weights = jnp.exp(scores - log_total).astype(jnp.bfloat16)
        context = jnp.einsum("hqk,khe->qhe", weights, value_seq, preferred_element_type=jnp.float32)
        return (context.astype(jnp.bfloat16), log_total[..., 0])

    context, log_total = lax.map(
        one_sequence, (shaped[0], shaped[1], shaped[2], labels.reshape(1, row_count))
    )
    return (context.reshape(row_count, local_width), log_total)


def attend_back(queries, key_rows, value_rows, labels, log_total, grad_context):
    row_count, local_width = queries.shape
    heads_here = local_width // HEAD_DIM
    shaped = [
        member.reshape(1, row_count, heads_here, HEAD_DIM)
        for member in (queries, key_rows, value_rows, grad_context)
    ]
    score_scale = HEAD_DIM ** (-0.5)

    def one_sequence(pieces):
        query_seq, key_seq, value_seq, label_seq, total_seq, grad_seq = pieces
        scores = masked_scores(query_seq, key_seq, label_seq)
        weights = jnp.exp(scores - total_seq[..., None])
        weights_low = weights.astype(jnp.bfloat16)
        grad_weights = jnp.einsum(
            "qhe,khe->hqk", grad_seq, value_seq, preferred_element_type=jnp.float32
        )
        inner_term = jnp.sum(weights * grad_weights, axis=-1, keepdims=True)
        grad_scores = (weights * (grad_weights - inner_term)).astype(jnp.bfloat16)
        grad_query = (
            jnp.einsum("hqk,khe->qhe", grad_scores, key_seq, preferred_element_type=jnp.float32)
            * score_scale
        )
        grad_keys = (
            jnp.einsum("hqk,qhe->khe", grad_scores, query_seq, preferred_element_type=jnp.float32)
            * score_scale
        )
        grad_values = jnp.einsum(
            "hqk,qhe->khe", weights_low, grad_seq, preferred_element_type=jnp.float32
        )
        return jnp.stack((grad_query, grad_keys, grad_values), axis=1).astype(jnp.bfloat16)

    stacked = lax.map(
        one_sequence,
        (shaped[0], shaped[1], shaped[2], labels.reshape(1, row_count), log_total, shaped[3]),
    )
    return stacked.reshape(row_count, 3, local_width)


def layer_forward(current, labels, weights, vectors):
    w_qkv, w_o, w_in, w_out = weights
    gains, biases, query_bias, value_bias, local_hidden_bias = vectors
    gathered = lax.all_gather(current, "tensor", axis=0, tiled=True)
    projected = jnp.einsum("gd,dcn->gcn", gathered, w_qkv, preferred_element_type=jnp.float32)
    queries = (projected[:, 0] + query_bias).astype(jnp.bfloat16)
    key_rows = projected[:, 1].astype(jnp.bfloat16)
    value_rows = (projected[:, 2] + value_bias).astype(jnp.bfloat16)
    context, log_total = attend(queries, key_rows, value_rows, labels)
    partial_value = jnp.dot(context, w_o, preferred_element_type=jnp.float32)
    mixed_rows = lax.psum_scatter(partial_value, "tensor", scatter_dimension=0, tiled=True)
    normed, scaled_one, inverse_one = norm_forward(
        current.astype(jnp.float32) + mixed_rows + biases[2], gains[0], biases[3]
    )
    spread_rows = lax.all_gather(normed.astype(jnp.bfloat16), "tensor", axis=0, tiled=True)
    hidden = jnp.dot(spread_rows, w_in, preferred_element_type=jnp.float32) + local_hidden_bias
    active = jax.nn.gelu(hidden, approximate=False).astype(jnp.bfloat16)
    partial_out = jnp.dot(active, w_out, preferred_element_type=jnp.float32)
    branch = lax.psum_scatter(
        partial_out.astype(jnp.bfloat16), "tensor", scatter_dimension=0, tiled=True
    ).astype(jnp.float32)
    final_rows, scaled_two, inverse_two = norm_forward(
        normed + branch + biases[4], gains[1], biases[5]
    )
    kept_state = (
        gathered,
        queries,
        key_rows,
        value_rows,
        context,
        log_total,
        scaled_one,
        inverse_one,
        spread_rows,
        hidden,
        active,
        scaled_two,
        inverse_two,
    )
    return (final_rows.astype(jnp.bfloat16), kept_state)


def layer_backward(upstream, kept_state, labels, weights, gains):
    (
        gathered,
        queries,
        key_rows,
        value_rows,
        context,
        log_total,
        scaled_one,
        inverse_one,
        spread_rows,
        hidden,
        active,
        scaled_two,
        inverse_two,
    ) = kept_state
    w_qkv, w_o, w_in, w_out = weights
    grad_second, gain_two, shift_two = norm_backward(upstream, scaled_two, inverse_two, gains[1])
    grad_feed = lax.all_gather(grad_second.astype(jnp.bfloat16), "tensor", axis=0, tiled=True)
    grad_active = dot_cols(grad_feed, w_out)
    grad_w_out = dot_rows(active, grad_feed)
    grad_hidden = (grad_active * gelu_slope(hidden)).astype(jnp.bfloat16)
    grad_w_in = dot_rows(spread_rows, grad_hidden)
    grad_spread = dot_cols(grad_hidden, w_in)
    grad_normed = grad_second + lax.psum_scatter(
        grad_spread.astype(jnp.bfloat16), "tensor", scatter_dimension=0, tiled=True
    ).astype(jnp.float32)
    grad_first, gain_one, shift_one = norm_backward(grad_normed, scaled_one, inverse_one, gains[0])
    grad_mix = lax.all_gather(grad_first.astype(jnp.bfloat16), "tensor", axis=0, tiled=True)
    grad_context = dot_cols(grad_mix, w_o).astype(jnp.bfloat16)
    grad_w_o = dot_rows(context, grad_mix)
    grad_project = attend_back(queries, key_rows, value_rows, labels, log_total, grad_context)
    grad_w_qkv = jnp.einsum(
        "gd,gcn->dcn", gathered, grad_project, preferred_element_type=jnp.float32
    )
    grad_gathered = jnp.einsum(
        "gcn,dcn->gd", grad_project, w_qkv, preferred_element_type=jnp.float32
    )
    grad_current = grad_first + lax.psum_scatter(
        grad_gathered.astype(jnp.bfloat16), "tensor", scatter_dimension=0, tiled=True
    ).astype(jnp.float32)
    column_sums = jnp.sum(grad_project.astype(jnp.float32), axis=0)
    gain_grads = jnp.stack([gain_one, gain_two])
    row_grads = jnp.stack(
        [jnp.sum(grad_first, axis=0), shift_one, jnp.sum(grad_second, axis=0), shift_two]
    )
    local_grads = jnp.stack([column_sums[0], column_sums[2]])
    hidden_grads = jnp.sum(grad_hidden.astype(jnp.float32), axis=0)
    return (
        grad_current,
        (grad_w_qkv, grad_w_o, grad_w_in, grad_w_out),
        (gain_grads, row_grads, local_grads, hidden_grads),
    )


def body(inputs, segments, cotangent, w_qkv, w_o, w_in, w_out, ln_gains, model_biases, hidden_bias):
    section_first = lax.axis_index("pipe") == 0
    column = lax.axis_index("tensor")
    micro_count = inputs.shape[0]
    row_count = inputs.shape[1]
    model_width = model_biases.shape[-1]
    hidden_width = hidden_bias.shape[-1]
    width_local = w_qkv.shape[-1]
    hidden_local = w_in.shape[-1]
    gains = ln_gains[0]
    biases = model_biases[0]
    query_bias = lax.dynamic_slice_in_dim(biases[0], column * width_local, width_local)
    value_bias = lax.dynamic_slice_in_dim(biases[1], column * width_local, width_local)
    local_hidden_bias = lax.dynamic_slice_in_dim(
        hidden_bias[0], column * hidden_local, hidden_local
    )
    vectors = (gains, biases, query_bias, value_bias, local_hidden_bias)
    shards = (w_qkv[0], w_o[0], w_in[0], w_out[0])
    blank_rows = jnp.zeros((row_count, model_width), jnp.bfloat16)
    incoming = blank_rows
    returning = blank_rows
    kept_list = []
    forward_list = []
    backward_list = []
    weight_totals = None
    vector_totals = None
    for tick_index in range(micro_count + 2):
        weights = (
            lax.all_gather(shards[0], "dp", axis=0, tiled=True),
            lax.all_gather(shards[1], "dp", axis=1, tiled=True),
            lax.all_gather(shards[2], "dp", axis=0, tiled=True),
            lax.all_gather(shards[3], "dp", axis=1, tiled=True),
        )
        own_rows = inputs[tick_index] if tick_index < micro_count else blank_rows
        current = jnp.where(section_first, own_rows, incoming)
        labels_forward = jnp.where(
            section_first,
            segments[min(tick_index, micro_count - 1)],
            segments[max(min(tick_index - 1, micro_count - 1), 0)],
        )
        final_rows, kept_state = layer_forward(current, labels_forward, weights, vectors)
        forward_list.append(final_rows)
        incoming = shifted(final_rows, "pipe", 1)
        given_grad = cotangent[tick_index - 1] if 1 <= tick_index <= micro_count else blank_rows
        upstream = jnp.where(section_first, returning, given_grad).astype(jnp.float32)
        earlier = kept_list[tick_index - 2] if tick_index >= 2 else kept_state
        chosen_state = jax.tree.map(
            lambda first_item, second_item: jnp.where(section_first, first_item, second_item),
            earlier,
            kept_state,
        )
        labels_backward = jnp.where(
            section_first,
            segments[max(min(tick_index - 2, micro_count - 1), 0)],
            segments[max(min(tick_index - 1, micro_count - 1), 0)],
        )
        grad_current, weight_grads, vector_grads = layer_backward(
            upstream, chosen_state, labels_backward, weights, gains
        )
        if tick_index == 0:
            weight_totals = weight_grads
            vector_totals = vector_grads
        else:
            weight_totals = jax.tree.map(jnp.add, weight_totals, weight_grads)
            vector_totals = jax.tree.map(jnp.add, vector_totals, vector_grads)
        grad_low = grad_current.astype(jnp.bfloat16)
        backward_list.append(grad_low)
        returning = shifted(grad_low, "pipe", -1)
        kept_list.append(kept_state)
    summed = (
        lax.psum_scatter(
            weight_totals[0].astype(jnp.bfloat16), "dp", scatter_dimension=0, tiled=True
        ).astype(jnp.float32),
        lax.psum_scatter(
            weight_totals[1].astype(jnp.bfloat16), "dp", scatter_dimension=1, tiled=True
        ).astype(jnp.float32),
        lax.psum_scatter(
            weight_totals[2].astype(jnp.bfloat16), "dp", scatter_dimension=0, tiled=True
        ).astype(jnp.float32),
        lax.psum_scatter(
            weight_totals[3].astype(jnp.bfloat16), "dp", scatter_dimension=1, tiled=True
        ).astype(jnp.float32),
    )
    gain_grads, row_grads, local_grads, hidden_grads = vector_totals
    zero_index = jnp.zeros((), jnp.int32)
    placed = lax.dynamic_update_slice(
        jnp.zeros((2, model_width), jnp.float32), local_grads, (zero_index, column * width_local)
    )
    bias_full = jnp.concatenate([placed, row_grads], axis=0)
    hidden_full = lax.dynamic_update_slice(
        jnp.zeros((hidden_width,), jnp.float32), hidden_grads, (column * hidden_local,)
    )
    vector_sums = (
        lax.psum_scatter(gain_grads, ("dp", "tensor"), scatter_dimension=1, tiled=True),
        lax.psum_scatter(bias_full, ("dp", "tensor"), scatter_dimension=1, tiled=True),
        lax.psum_scatter(hidden_full, ("dp", "tensor"), scatter_dimension=0, tiled=True),
    )
    section_rows = jnp.stack(
        [
            jnp.where(section_first, forward_list[batch_index], forward_list[batch_index + 1])
            for batch_index in range(micro_count)
        ]
    )[None]
    grad_rows = jnp.stack(
        [
            jnp.where(section_first, backward_list[batch_index + 2], backward_list[batch_index + 1])
            for batch_index in range(micro_count)
        ]
    )[None]
    return (
        section_rows,
        grad_rows,
        summed[0][None],
        summed[1][None],
        summed[2][None],
        summed[3][None],
        vector_sums[0][None],
        vector_sums[1][None],
        vector_sums[2][None],
    )


def solution(mesh):
    return jax.shard_map(
        body,
        mesh=mesh,
        in_specs=(
            P(None, ("dp", "tensor"), None),
            P(None, "dp"),
            P(None, ("dp", "tensor"), None),
            P("pipe", "dp", None, "tensor"),
            P("pipe", "tensor", "dp"),
            P("pipe", "dp", "tensor"),
            P("pipe", "tensor", "dp"),
            P("pipe", None, None),
            P("pipe", None, None),
            P("pipe", None),
        ),
        out_specs=(
            P("pipe", None, ("dp", "tensor"), None),
            P("pipe", None, ("dp", "tensor"), None),
            P("pipe", "dp", None, "tensor"),
            P("pipe", "tensor", "dp"),
            P("pipe", "dp", "tensor"),
            P("pipe", "tensor", "dp"),
            P("pipe", None, ("dp", "tensor")),
            P("pipe", None, ("dp", "tensor")),
            P("pipe", ("dp", "tensor")),
        ),
        check_vma=False,
    )
```

profile of v0, /device:TPU:0, one launch (start us, length us, event | category | flops | bytes accessed | tf_op | source)
XLA Modules:
  0.0 1325.6 jit_solution(16337392418680728141)
XLA Ops:
  11.8 17.4 %all-gather = bf16[1,256,1024]{2,1,0:T(8,128)(2,1)S(1)} all-gather(bf16[1,64,1024]{2,1,0:T(8,128)(2,1)S(1)} %slice_select_fusion), channel_id=2, replica_groups=mesh['pipe'=2,'dp'=4,'tensor'=4] {'tensor'}, dimensions={1}, use_global_device_ids=true | all-gather | bytes 655360 | tf_op jit(solution)/shard_map/all_gather | solution.py:131
  43.2 27.1 %reduce-scatter.35.cloned.1.call-done = f32[64,1024]{1,0:T(8,128)} async-done(((f32[256,1024]{1,0:T(8,128)}), f32[64,1024]{1,0:T(8,128)}) %reduce-scatter.35.cloned.1.call-update) | async-done | bytes 262160 | tf_op jit(solution)/shard_map/reduce_scatter | solution.py:138
  73.6 16.0 %all_gather.107 = bf16[256,1024]{1,0:T(8,128)(2,1)S(1)} all-gather(bf16[64,1024]{1,0:T(8,128)(2,1)S(1)} %get-tuple-element.418), channel_id=1, replica_groups=mesh['pipe'=2,'dp'=4,'tensor'=4] {'tensor'}, dimensions={0}, use_global_device_ids=true | all-gather | bytes 655360 | tf_op jit(solution)/shard_map/all_gather | solution.py:142
  98.4 18.8 %all-gather.13.cloned.1.call-done = bf16[1,1024,1024]{2,1,0:T(8,128)(2,1)} async-done(((bf16[1,1024,256]{2,1,0:T(8,128)(2,1)}), bf16[1,1024,1024]{2,1,0:T(8,128)(2,1)}) %all-gather.13.cloned.1.call-update) | async-done | bytes 2097168 | tf_op jit(solution)/shard_map/all_gather | solution.py:256
  121.6 20.6 %reduce-scatter.37.cloned.1.call-done = bf16[64,1024]{1,0:T(8,128)(2,1)} async-done(((bf16[256,1024]{1,0:T(8,128)(2,1)}), bf16[64,1024]{1,0:T(8,128)(2,1)}) %reduce-scatter.37.cloned.1.call-update) | async-done | bytes 131088 | tf_op jit(solution)/shard_map/reduce_scatter | solution.py:146
  145.9 15.4 %all_gather.118 = bf16[256,1024]{1,0:T(8,128)(2,1)S(1)} all-gather(bf16[64,1024]{1,0:T(8,128)(2,1)S(1)} %fusion.434), channel_id=1, replica_groups=mesh['pipe'=2,'dp'=4,'tensor'=4] {'tensor'}, dimensions={0}, use_global_device_ids=true | all-gather | bytes 655360 | tf_op jit(solution)/shard_map/all_gather | solution.py:188
  167.5 19.8 %reduce-scatter.55.cloned.1.call-done = bf16[64,1024]{1,0:T(8,128)(2,1)} async-done(((bf16[256,1024]{1,0:T(8,128)(2,1)}), bf16[64,1024]{1,0:T(8,128)(2,1)}) %reduce-scatter.55.cloned.1.call-update) | async-done | bytes 131088 | tf_op jit(solution)/shard_map/reduce_scatter | solution.py:194
  196.6 14.8 %all_gather.110 = bf16[256,1024]{1,0:T(8,128)(2,1)S(1)} all-gather(bf16[64,1024]{1,0:T(8,128)(2,1)S(1)} %bitcast_select_fusion.8), channel_id=1, replica_groups=mesh['pipe'=2,'dp'=4,'tensor'=4] {'tensor'}, dimensions={0}, use_global_device_ids=true | all-gather | bytes 655360 | tf_op jit(solution)/shard_map/all_gather | solution.py:131
  218.2 26.0 %reduce-scatter.39.cloned.1.call-done = f32[64,1024]{1,0:T(8,128)} async-done(((f32[256,1024]{1,0:T(8,128)}), f32[64,1024]{1,0:T(8,128)}) %reduce-scatter.39.cloned.1.call-update) | async-done | bytes 262160 | tf_op jit(solution)/shard_map/reduce_scatter | solution.py:138
  249.5 16.1 %all_gather.119 = bf16[256,1024]{1,0:T(8,128)(2,1)S(1)} all-gather(bf16[64,1024]{1,0:T(8,128)(2,1)S(1)} %convert_element_type.638), channel_id=1, replica_groups=mesh['pipe'=2,'dp'=4,'tensor'=4] {'tensor'}, dimensions={0}, use_global_device_ids=true | all-gather | bytes 655360 | tf_op jit(solution)/shard_map/all_gather | solution.py:198
  268.9 15.6 %all_gather.111 = bf16[256,1024]{1,0:T(8,128)(2,1)S(1)} all-gather(bf16[64,1024]{1,0:T(8,128)(2,1)S(1)} %get-tuple-element.478), channel_id=1, replica_groups=mesh['pipe'=2,'dp'=4,'tensor'=4] {'tensor'}, dimensions={0}, use_global_device_ids=true | all-gather | bytes 655360 | tf_op jit(solution)/shard_map/all_gather | solution.py:142
  298.1 13.0 reduce-scatter.41.cloned.1.call-done
  317.2 16.9 %reduce-scatter.57.cloned.1.call-done = bf16[64,1024]{1,0:T(8,128)(2,1)} async-done(((bf16[256,1024]{1,0:T(8,128)(2,1)}), bf16[64,1024]{1,0:T(8,128)(2,1)}) %reduce-scatter.57.cloned.1.call-update) | async-done | bytes 131088 | tf_op jit(solution)/shard_map/reduce_scatter | solution.py:208
  337.3 15.3 %all_gather.112 = bf16[256,1024]{1,0:T(8,128)(2,1)S(1)} all-gather(bf16[64,1024]{1,0:T(8,128)(2,1)S(1)} %bitcast_select_fusion.7), channel_id=1, replica_groups=mesh['pipe'=2,'dp'=4,'tensor'=4] {'tensor'}, dimensions={0}, use_global_device_ids=true | all-gather | bytes 655360 | tf_op jit(solution)/shard_map/all_gather | solution.py:131
  356.9 15.8 %all_gather.120 = bf16[256,1024]{1,0:T(8,128)(2,1)S(1)} all-gather(bf16[64,1024]{1,0:T(8,128)(2,1)S(1)} %get-tuple-element.388), channel_id=1, replica_groups=mesh['pipe'=2,'dp'=4,'tensor'=4] {'tensor'}, dimensions={0}, use_global_device_ids=true | all-gather | bytes 655360 | tf_op jit(solution)/shard_map/all_gather | solution.py:188
  385.3 12.8 reduce-scatter.59.cloned.1.call-done
  399.7 26.3 %reduce-scatter.43.cloned.1.call-done = f32[64,1024]{1,0:T(8,128)} async-done(((f32[256,1024]{1,0:T(8,128)}), f32[64,1024]{1,0:T(8,128)}) %reduce-scatter.43.cloned.1.call-update) | async-done | bytes 262160 | tf_op jit(solution)/shard_map/reduce_scatter | solution.py:138
  429.8 16.1 %all_gather.113 = bf16[256,1024]{1,0:T(8,128)(2,1)S(1)} all-gather(bf16[64,1024]{1,0:T(8,128)(2,1)S(1)} %get-tuple-element.477), channel_id=1, replica_groups=mesh['pipe'=2,'dp'=4,'tensor'=4] {'tensor'}, dimensions={0}, use_global_device_ids=true | all-gather | bytes 655360 | tf_op jit(solution)/shard_map/all_gather | solution.py:142
  453.3 17.9 %all_gather.121 = bf16[256,1024]{1,0:T(8,128)(2,1)S(1)} all-gather(bf16[64,1024]{1,0:T(8,128)(2,1)S(1)} %convert_element_type.649), channel_id=1, replica_groups=mesh['pipe'=2,'dp'=4,'tensor'=4] {'tensor'}, dimensions={0}, use_global_device_ids=true | all-gather | bytes 655360 | tf_op jit(solution)/shard_map/all_gather | solution.py:198
  490.7 17.9 %all_gather.114 = bf16[256,1024]{1,0:T(8,128)(2,1)S(1)} all-gather(bf16[64,1024]{1,0:T(8,128)(2,1)S(1)} %bitcast_select_fusion.6), channel_id=1, replica_groups=mesh['pipe'=2,'dp'=4,'tensor'=4] {'tensor'}, dimensions={0}, use_global_device_ids=true | all-gather | bytes 655360 | tf_op jit(solution)/shard_map/all_gather | solution.py:131
  524.6 20.5 %all_gather.122 = bf16[256,1024]{1,0:T(8,128)(2,1)S(1)} all-gather(bf16[64,1024]{1,0:T(8,128)(2,1)S(1)} %get-tuple-element.384), channel_id=1, replica_groups=mesh['pipe'=2,'dp'=4,'tensor'=4] {'tensor'}, dimensions={0}, use_global_device_ids=true | all-gather | bytes 655360 | tf_op jit(solution)/shard_map/all_gather | solution.py:188
  552.1 20.5 %reduce-scatter.63.cloned.1.call-done = bf16[64,1024]{1,0:T(8,128)(2,1)} async-done(((bf16[256,1024]{1,0:T(8,128)(2,1)}), bf16[64,1024]{1,0:T(8,128)(2,1)}) %reduce-scatter.63.cloned.1.call-update) | async-done | bytes 131088 | tf_op jit(solution)/shard_map/reduce_scatter | solution.py:194
  575.2 15.5 %all_gather.115 = bf16[256,1024]{1,0:T(8,128)(2,1)S(1)} all-gather(bf16[64,1024]{1,0:T(8,128)(2,1)S(1)} %get-tuple-element.476), channel_id=1, replica_groups=mesh['pipe'=2,'dp'=4,'tensor'=4] {'tensor'}, dimensions={0}, use_global_device_ids=true | all-gather | bytes 655360 | tf_op jit(solution)/shard_map/all_gather | solution.py:142
  597.4 19.9 %reduce-scatter.49.cloned.1.call-done = bf16[64,1024]{1,0:T(8,128)(2,1)} async-done(((bf16[256,1024]{1,0:T(8,128)(2,1)}), bf16[64,1024]{1,0:T(8,128)(2,1)}) %reduce-scatter.49.cloned.1.call-update) | async-done | bytes 131088 | tf_op jit(solution)/shard_map/reduce_scatter | solution.py:146
  627.3 14.7 %all_gather.116 = bf16[256,1024]{1,0:T(8,128)(2,1)S(1)} all-gather(bf16[64,1024]{1,0:T(8,128)(2,1)S(1)} %broadcast_select_fusion.10), channel_id=1, replica_groups=mesh['pipe'=2,'dp'=4,'tensor'=4] {'tensor'}, dimensions={0}, use_global_device_ids=true | all-gather | bytes 655360 | tf_op jit(solution)/shard_map/all_gather | solution.py:131
  645.9 27.4 %reduce-scatter.51.cloned.1.call-done = f32[64,1024]{1,0:T(8,128)} async-done(((f32[256,1024]{1,0:T(8,128)}), f32[64,1024]{1,0:T(8,128)}) %reduce-scatter.51.cloned.1.call-update) | async-done | bytes 262160 | tf_op jit(solution)/shard_map/reduce_scatter | solution.py:138
  676.1 16.0 %all_gather.117 = bf16[256,1024]{1,0:T(8,128)(2,1)S(1)} all-gather(bf16[64,1024]{1,0:T(8,128)(2,1)S(1)} %get-tuple-element.475), channel_id=1, replica_groups=mesh['pipe'=2,'dp'=4,'tensor'=4] {'tensor'}, dimensions={0}, use_global_device_ids=true | all-gather | bytes 655360 | tf_op jit(solution)/shard_map/all_gather | solution.py:142
  699.3 18.1 %all_gather.123 = bf16[256,1024]{1,0:T(8,128)(2,1)S(1)} all-gather(bf16[64,1024]{1,0:T(8,128)(2,1)S(1)} %convert_element_type.661), channel_id=1, replica_groups=mesh['pipe'=2,'dp'=4,'tensor'=4] {'tensor'}, dimensions={0}, use_global_device_ids=true | all-gather | bytes 655360 | tf_op jit(solution)/shard_map/all_gather | solution.py:198
  737.1 17.8 %all_gather.128 = bf16[256,1024]{1,0:T(8,128)(2,1)S(1)} all-gather(bf16[64,1024]{1,0:T(8,128)(2,1)S(1)} %broadcast_select_fusion.9), channel_id=1, replica_groups=mesh['pipe'=2,'dp'=4,'tensor'=4] {'tensor'}, dimensions={0}, use_global_device_ids=true | all-gather | bytes 655360 | tf_op jit(solution)/shard_map/all_gather | solution.py:131
  770.6 21.0 %all_gather.124 = bf16[256,1024]{1,0:T(8,128)(2,1)S(1)} all-gather(bf16[64,1024]{1,0:T(8,128)(2,1)S(1)} %get-tuple-element.377), channel_id=1, replica_groups=mesh['pipe'=2,'dp'=4,'tensor'=4] {'tensor'}, dimensions={0}, use_global_device_ids=true | all-gather | bytes 655360 | tf_op jit(solution)/shard_map/all_gather | solution.py:188
  799.2 19.4 %reduce-scatter.67.cloned.1.call-done = bf16[64,1024]{1,0:T(8,128)(2,1)} async-done(((bf16[256,1024]{1,0:T(8,128)(2,1)}), bf16[64,1024]{1,0:T(8,128)(2,1)}) %reduce-scatter.67.cloned.1.call-update) | async-done | bytes 131088 | tf_op jit(solution)/shard_map/reduce_scatter | solution.py:194
  823.5 15.5 %all_gather.125 = bf16[256,1024]{1,0:T(8,128)(2,1)S(1)} all-gather(bf16[64,1024]{1,0:T(8,128)(2,1)S(1)} %convert_element_type.673), channel_id=1, replica_groups=mesh['pipe'=2,'dp'=4,'tensor'=4] {'tensor'}, dimensions={0}, use_global_device_ids=true | all-gather | bytes 655360 | tf_op jit(solution)/shard_map/all_gather | solution.py:198
  848.5 18.3 %all_gather.129 = bf16[256,1024]{1,0:T(8,128)(2,1)S(1)} all-gather(bf16[64,1024]{1,0:T(8,128)(2,1)} %get-tuple-element.464), channel_id=1, replica_groups=mesh['pipe'=2,'dp'=4,'tensor'=4] {'tensor'}, dimensions={0}, use_global_device_ids=true | all-gather | bytes 655360 | tf_op jit(solution)/shard_map/all_gather | solution.py:142
  882.7 20.5 %all_gather.126 = bf16[256,1024]{1,0:T(8,128)(2,1)S(1)} all-gather(bf16[64,1024]{1,0:T(8,128)(2,1)S(1)} %get-tuple-element.370), channel_id=1, replica_groups=mesh['pipe'=2,'dp'=4,'tensor'=4] {'tensor'}, dimensions={0}, use_global_device_ids=true | all-gather | bytes 655360 | tf_op jit(solution)/shard_map/all_gather | solution.py:188
  918.8 13.2 reduce-scatter.71.cloned.1.call-done
  937.3 15.7 %all_gather.127 = bf16[256,1024]{1,0:T(8,128)(2,1)S(1)} all-gather(bf16[64,1024]{1,0:T(8,128)(2,1)S(1)} %convert_element_type.685), channel_id=1, replica_groups=mesh['pipe'=2,'dp'=4,'tensor'=4] {'tensor'}, dimensions={0}, use_global_device_ids=true | all-gather | bytes 655360 | tf_op jit(solution)/shard_map/all_gather | solution.py:198
  971.6 12.3 reduce-scatter.73.cloned.1.call-done
  994.4 14.8 %all_gather.130 = bf16[256,1024]{1,0:T(8,128)(2,1)S(1)} all-gather(bf16[64,1024]{1,0:T(8,128)(2,1)S(1)} %get-tuple-element.360), channel_id=1, replica_groups=mesh['pipe'=2,'dp'=4,'tensor'=4] {'tensor'}, dimensions={0}, use_global_device_ids=true | all-gather | bytes 655360 | tf_op jit(solution)/shard_map/all_gather | solution.py:188
  1020.7 14.0 %reduce-scatter.79.cloned.1.call-done = bf16[64,1024]{1,0:T(8,128)(2,1)} async-done(((bf16[256,1024]{1,0:T(8,128)(2,1)}), bf16[64,1024]{1,0:T(8,128)(2,1)}) %reduce-scatter.79.cloned.1.call-update) | async-done | bytes 131088 | tf_op jit(solution)/shard_map/reduce_scatter | solution.py:194
  1038.1 15.6 %all_gather.131 = bf16[256,1024]{1,0:T(8,128)(2,1)S(1)} all-gather(bf16[64,1024]{1,0:T(8,128)(2,1)S(1)} %convert_element_type.708), channel_id=1, replica_groups=mesh['pipe'=2,'dp'=4,'tensor'=4] {'tensor'}, dimensions={0}, use_global_device_ids=true | all-gather | bytes 655360 | tf_op jit(solution)/shard_map/all_gather | solution.py:198
  1073.7 7.3 add_convert_fusion.1
  1103.6 57.9 %all-reduce = f32[4096]{0:T(1024)S(1)} all-reduce(f32[4096]{0:T(1024)S(1)} %add_dynamic-update-slice_fusion), channel_id=37, replica_groups=mesh['pipe'=2,'dp'=4,'tensor'=4] {'dp','tensor'}, use_global_device_ids=true, to_apply=%region_143.144.clone | all-reduce | flops 4096 | bytes 32768
  1163.5 8.3 reduce-scatter.93.cloned.1.call-done
  1173.2 22.3 %reduce-scatter.81.cloned.1.call-done = bf16[64,1024]{1,0:T(8,128)(2,1)} async-done(((bf16[256,1024]{1,0:T(8,128)(2,1)}), bf16[64,1024]{1,0:T(8,128)(2,1)}) %reduce-scatter.81.cloned.1.call-update) | async-done | bytes 131088 | tf_op jit(solution)/shard_map/reduce_scatter | solution.py:208
  1197.4 21.0 %reduce-scatter.85.cloned.1.call-done = bf16[256,256]{1,0:T(8,128)(2,1)} async-done(((bf16[256,1024]{1,0:T(8,128)(2,1)}), bf16[256,256]{1,0:T(8,128)(2,1)}) %reduce-scatter.85.cloned.1.call-update) | async-done | bytes 131088 | tf_op jit(solution)/shard_map/reduce_scatter | solution.py:298
  1220.1 32.1 %reduce-scatter.87.cloned.1.call-done = bf16[256,1024]{1,0:T(8,128)(2,1)} async-done(((bf16[1024,1024]{1,0:T(8,128)(2,1)}), bf16[256,1024]{1,0:T(8,128)(2,1)}) %reduce-scatter.87.cloned.1.call-update) | async-done | bytes 524304 | tf_op jit(solution)/shard_map/reduce_scatter | solution.py:301
  1254.3 31.6 %reduce-scatter.89.cloned.1.call-done = bf16[1024,256]{1,0:T(8,128)(2,1)} async-done(((bf16[1024,1024]{1,0:T(8,128)(2,1)}), bf16[1024,256]{1,0:T(8,128)(2,1)}) %reduce-scatter.89.cloned.1.call-update) | async-done | bytes 524304 | tf_op jit(solution)/shard_map/reduce_scatter | solution.py:304
  1288.0 28.4 %reduce-scatter.83.cloned.1.call-done = bf16[256,3,256]{2,0,1:T(8,128)(2,1)} async-done(((bf16[1024,3,256]{2,0,1:T(8,128)(2,1)}), bf16[256,3,256]{2,0,1:T(8,128)(2,1)}) %reduce-scatter.83.cloned.1.call-update) | async-done | bytes 393232 | tf_op jit(solution)/shard_map/reduce_scatter | solution.py:295
  (1195 shorter events, 386.0 us)
Async XLA Ops:
  7.2 29.9 %all-gather.9.cloned.1.call-start = ((), (), s32[]{:S(2)}) async-start(), calls=%async_computation.58 | async-start | bytes 1966080 | tf_op jit(solution)/shard_map/all_gather | solution.py:253
  9.2 61.0 %reduce-scatter.35.cloned.1.call-start = ((), (), s32[]{:S(2)}) async-start(), calls=%async_computation.30 | async-start | bytes 1310720 | tf_op jit(solution)/shard_map/reduce_scatter | solution.py:138
  10.7 134.0 %copy-start.245 = (f32[1,1,1024]{2,0,1:T(1,128)}, f32[1,1,1024]{2,0,1:T(1,128)S(1)}, u32[]{:S(2)}) copy-start(f32[1,1,1024]{2,0,1:T(1,128)S(1)} %get-tuple-element.443) | copy-start | bytes 12292
  41.8 51.2 %all-gather.11.cloned.1.call-start = ((), (), s32[]{:S(2)}) async-start(), calls=%async_computation.59 | async-start | bytes 2621440 | tf_op jit(solution)/shard_map/all_gather | solution.py:255
  42.5 74.7 %all-gather.13.cloned.1.call-start = ((), (), s32[]{:S(2)}) async-start(), calls=%async_computation.60 | async-start | bytes 2621440 | tf_op jit(solution)/shard_map/all_gather | solution.py:256
  43.1 99.2 %reduce-scatter.37.cloned.1.call-start = ((), (), s32[]{:S(2)}) async-start(), calls=%async_computation.31 | async-start | bytes 655360 | tf_op jit(solution)/shard_map/reduce_scatter | solution.py:146
  120.3 66.9 %reduce-scatter.55.cloned.1.call-start = ((), (), s32[]{:S(2)}) async-start(), calls=%async_computation.40 | async-start | bytes 655360 | tf_op jit(solution)/shard_map/reduce_scatter | solution.py:194
  166.8 77.3 %reduce-scatter.39.cloned.1.call-start = ((), (), s32[]{:S(2)}) async-start(), calls=%async_computation.32 | async-start | bytes 1310720 | tf_op jit(solution)/shard_map/reduce_scatter | solution.py:138
  189.9 5.8 collective-permute-start
  216.7 94.4 %reduce-scatter.41.cloned.1.call-start = ((), (), s32[]{:S(2)}) async-start(), calls=%async_computation.33 | async-start | bytes 655360 | tf_op jit(solution)/shard_map/reduce_scatter | solution.py:146
  290.8 43.3 %reduce-scatter.57.cloned.1.call-start = ((), (), s32[]{:S(2)}) async-start(), calls=%async_computation.41 | async-start | bytes 655360 | tf_op jit(solution)/shard_map/reduce_scatter | solution.py:208
  298.1 100.0 %reduce-scatter.59.cloned.1.call-start = ((), (), s32[]{:S(2)}) async-start(), calls=%async_computation.42 | async-start | bytes 655360 | tf_op jit(solution)/shard_map/reduce_scatter | solution.py:194
  314.0 22.4 %collective-permute-start.1 = (bf16[64,1024]{1,0:T(8,128)(2,1)S(1)}, bf16[64,1024]{1,0:T(8,128)(2,1)S(1)}, u32[]{:S(2)}, u32[]{:S(2)}) collective-permute-start(bf16[64,1024]{1,0:T(8,128)(2,1)S(1)} %get-tuple-element.395), channel_id=1, source_target_pairs={{0,16},{1,17},{2,18},{3,19},{4,20},{5,21},{6,22},{7,23},{8,24},{9,... | collective-permute-start | bytes 393224 | tf_op jit(solution)/shard_map/ppermute | solution.py:18
  335.1 19.1 %collective-permute-start.4 = (bf16[64,1024]{1,0:T(8,128)(2,1)S(1)}, bf16[64,1024]{1,0:T(8,128)(2,1)S(1)}, u32[]{:S(2)}, u32[]{:S(2)}) collective-permute-start(bf16[64,1024]{1,0:T(8,128)(2,1)S(1)} %add_convert_fusion.10), channel_id=1, source_target_pairs={{16,0},{17,1},{18,2},{19,3},{20,4},{21,5},{22,6},{23,7},{24,8},{25... | collective-permute-start | bytes 393224 | tf_op jit(solution)/shard_map/ppermute | solution.py:18
  376.7 49.4 %reduce-scatter.43.cloned.1.call-start = ((), (), s32[]{:S(2)}) async-start(), calls=%async_computation.34 | async-start | bytes 1310720 | tf_op jit(solution)/shard_map/reduce_scatter | solution.py:138
  383.8 95.7 %reduce-scatter.45.cloned.1.call-start = ((), (), s32[]{:S(2)}) async-start(), calls=%async_computation.35 | async-start | bytes 655360 | tf_op jit(solution)/shard_map/reduce_scatter | solution.py:146
  452.2 61.9 %reduce-scatter.61.cloned.1.call-start = ((), (), s32[]{:S(2)}) async-start(), calls=%async_computation.43 | async-start | bytes 655360 | tf_op jit(solution)/shard_map/reduce_scatter | solution.py:208
  483.8 6.0 collective-permute-start.2
  488.7 62.0 %reduce-scatter.47.cloned.1.call-start = ((), (), s32[]{:S(2)}) async-start(), calls=%async_computation.36 | async-start | bytes 1310720 | tf_op jit(solution)/shard_map/reduce_scatter | solution.py:138
  514.0 58.5 %reduce-scatter.63.cloned.1.call-start = ((), (), s32[]{:S(2)}) async-start(), calls=%async_computation.44 | async-start | bytes 655360 | tf_op jit(solution)/shard_map/reduce_scatter | solution.py:194
  515.3 6.9 collective-permute-start.5
  550.6 66.7 %reduce-scatter.49.cloned.1.call-start = ((), (), s32[]{:S(2)}) async-start(), calls=%async_computation.37 | async-start | bytes 655360 | tf_op jit(solution)/shard_map/reduce_scatter | solution.py:146
  597.0 76.3 %reduce-scatter.51.cloned.1.call-start = ((), (), s32[]{:S(2)}) async-start(), calls=%async_computation.38 | async-start | bytes 1310720 | tf_op jit(solution)/shard_map/reduce_scatter | solution.py:138
  620.8 5.8 collective-permute-start.3
  645.8 82.1 %reduce-scatter.53.cloned.1.call-start = ((), (), s32[]{:S(2)}) async-start(), calls=%async_computation.39 | async-start | bytes 655360 | tf_op jit(solution)/shard_map/reduce_scatter | solution.py:146
  699.2 60.3 %reduce-scatter.65.cloned.1.call-start = ((), (), s32[]{:S(2)}) async-start(), calls=%async_computation.45 | async-start | bytes 655360 | tf_op jit(solution)/shard_map/reduce_scatter | solution.py:208
  730.7 5.8 collective-permute-start.8
  735.4 61.3 %reduce-scatter.75.cloned.1.call-start = ((), (), s32[]{:S(2)}) async-start(), calls=%async_computation.50 | async-start | bytes 1310720 | tf_op jit(solution)/shard_map/reduce_scatter | solution.py:138
  759.4 59.3 %reduce-scatter.67.cloned.1.call-start = ((), (), s32[]{:S(2)}) async-start(), calls=%async_computation.46 | async-start | bytes 655360 | tf_op jit(solution)/shard_map/reduce_scatter | solution.py:194
  761.2 6.8 collective-permute-start.6
  795.0 75.3 %reduce-scatter.69.cloned.1.call-start = ((), (), s32[]{:S(2)}) async-start(), calls=%async_computation.47 | async-start | bytes 655360 | tf_op jit(solution)/shard_map/reduce_scatter | solution.py:208
  847.8 71.1 %reduce-scatter.77.cloned.1.call-start = ((), (), s32[]{:S(2)}) async-start(), calls=%async_computation.51 | async-start | bytes 655360 | tf_op jit(solution)/shard_map/reduce_scatter | solution.py:146
  871.9 7.3 collective-permute-start.7
  878.9 53.2 %reduce-scatter.71.cloned.1.call-start = ((), (), s32[]{:S(2)}) async-start(), calls=%async_computation.48 | async-start | bytes 655360 | tf_op jit(solution)/shard_map/reduce_scatter | solution.py:194
  909.4 74.4 %reduce-scatter.73.cloned.1.call-start = ((), (), s32[]{:S(2)}) async-start(), calls=%async_computation.49 | async-start | bytes 655360 | tf_op jit(solution)/shard_map/reduce_scatter | solution.py:208
  963.5 71.2 %reduce-scatter.79.cloned.1.call-start = ((), (), s32[]{:S(2)}) async-start(), calls=%async_computation.52 | async-start | bytes 655360 | tf_op jit(solution)/shard_map/reduce_scatter | solution.py:194
  985.7 6.8 collective-permute-start.9
  1014.8 147.3 %reduce-scatter.91.cloned.1.call-start = ((), (), s32[]{:S(2)}) async-start(), calls=%async_computation.61 | async-start | bytes 557056
  1058.4 113.5 %reduce-scatter.93.cloned.1.call-start = ((), (), s32[]{:S(2)}) async-start(), calls=%async_computation.62 | async-start | bytes 557056
  1061.3 134.2 %reduce-scatter.81.cloned.1.call-start = ((), (), s32[]{:S(2)}) async-start(), calls=%async_computation.53 | async-start | bytes 655360 | tf_op jit(solution)/shard_map/reduce_scatter | solution.py:208
  1063.9 154.5 %reduce-scatter.85.cloned.1.call-start = ((), (), s32[]{:S(2)}) async-start(), calls=%async_computation.55 | async-start | bytes 655360 | tf_op jit(solution)/shard_map/reduce_scatter | solution.py:298
  1071.0 181.2 %reduce-scatter.87.cloned.1.call-start = ((), (), s32[]{:S(2)}) async-start(), calls=%async_computation.56 | async-start | bytes 2621440 | tf_op jit(solution)/shard_map/reduce_scatter | solution.py:301
  1081.1 204.8 %reduce-scatter.89.cloned.1.call-start = ((), (), s32[]{:S(2)}) async-start(), calls=%async_computation.57 | async-start | bytes 2621440 | tf_op jit(solution)/shard_map/reduce_scatter | solution.py:304
  1092.7 223.7 %reduce-scatter.83.cloned.1.call-start = ((), (), s32[]{:S(2)}) async-start(), calls=%async_computation.54 | async-start | bytes 1966080 | tf_op jit(solution)/shard_map/reduce_scatter | solution.py:295
  1101.3 95.2 %copy-start.242 = (bf16[1,64,1024]{2,1,0:T(8,128)(2,1)S(1)}, bf16[1,64,1024]{2,1,0:T(8,128)(2,1)}, u32[]{:S(2)}) copy-start(bf16[1,64,1024]{2,1,0:T(8,128)(2,1)} %get-tuple-element.335) | copy-start | bytes 393220
  1101.3 95.2 %copy-start.243 = (bf16[1,64,1024]{2,1,0:T(8,128)(2,1)S(1)}, bf16[1,64,1024]{2,1,0:T(8,128)(2,1)}, u32[]{:S(2)}) copy-start(bf16[1,64,1024]{2,1,0:T(8,128)(2,1)} %get-tuple-element.345) | copy-start | bytes 393220
  1101.3 95.2 %copy-start.244 = (bf16[1,64,1024]{2,1,0:T(8,128)(2,1)S(1)}, bf16[1,64,1024]{2,1,0:T(8,128)(2,1)}, u32[]{:S(2)}) copy-start(bf16[1,64,1024]{2,1,0:T(8,128)(2,1)} %get-tuple-element.347) | copy-start | bytes 393220
  1218.4 99.9 %copy-start.1 = (f32[1,4096]{1,0:T(1,128)S(1)}, f32[1,4096]{1,0:T(1,128)}, u32[]{:S(2)}) copy-start(f32[1,4096]{1,0:T(1,128)} %param.19) | copy-start | bytes 49156
  (376 other events, 3893.9 us)
Sparse Core Ops, SparseCore 0:
  10.1 22.6 all-gather.8
  41.9 28.3 reduce-scatter.34
  71.8 21.0 all-gather.10
  94.3 22.8 all-gather.12
  120.4 21.8 reduce-scatter.36
  166.9 20.2 reduce-scatter.54
  216.9 27.2 reduce-scatter.38
  290.9 20.1 reduce-scatter.40
  314.0 20.0 reduce-scatter.56
  376.8 21.2 reduce-scatter.58
  400.4 25.5 reduce-scatter.42
  452.4 22.3 reduce-scatter.44
  488.8 21.2 reduce-scatter.60
  514.2 35.1 reduce-scatter.46
  552.1 20.4 reduce-scatter.62
  597.1 20.1 reduce-scatter.48
  645.9 27.3 reduce-scatter.50
  699.3 21.8 reduce-scatter.52
  735.5 21.1 reduce-scatter.64
  759.5 35.9 reduce-scatter.74
  798.3 20.2 reduce-scatter.66
  847.9 21.7 reduce-scatter.68
  879.0 25.8 reduce-scatter.76
  909.5 22.4 reduce-scatter.70
  963.6 20.1 reduce-scatter.72
  1014.9 19.7 reduce-scatter.78
  1058.5 54.5 reduce-scatter.90
  1116.6 55.1 reduce-scatter.92
  1174.7 20.8 reduce-scatter.80
  1198.5 19.9 reduce-scatter.84
  1220.9 31.1 reduce-scatter.86
  1254.7 31.1 reduce-scatter.88
  1288.3 28.0 reduce-scatter.82
where the time goes:
time: 1340 us; the launch traced here: 1330 us
  waiting for transfers between devices  478 us (36%)
  blocking collectives  467 us (35%)
  matrix products  163 us (12%)
  other arithmetic  113 us (8%)
  local copies, waits for them, and re-layouts  58.1 us (4%)
  starting transfers between devices  25.5 us (2%)
  between operations  20.5 us (2%)
    all_gather x6, blocking collectives, layer_backward(): lax.all_gather(grad_second.astype(jnp.bfloat16), 'tensor', axis=0, tiled=...  108 us
    reduce_scatter x6, waiting for transfers between devices, layer_forward(): lax.psum_scatter(partial_value, 'tensor', scatter_dimension=0, tiled=True)  107 us
    reduce_scatter x6, waiting for transfers between devices, layer_backward(): lax.psum_scatter(grad_spread.astype(jnp.bfloat16), 'tensor', scatter_dime...  99.6 us
    all_gather x6, blocking collectives, layer_backward(): lax.all_gather(grad_first.astype(jnp.bfloat16), 'tensor', axis=0, tiled=T...  98.8 us
    all_gather x6, blocking collectives, layer_forward(): gathered = lax.all_gather(current, 'tensor', axis=0, tiled=True)  97.9 us
    all_gather x6, blocking collectives, layer_forward(): lax.all_gather(normed.astype(jnp.bfloat16), 'tensor', axis=0, tiled=True)  97.5 us
    unnamed x1, blocking collectives  57.9 us
    reduce_scatter x6, waiting for transfers between devices, layer_forward(): lax.psum_scatter(partial_out.astype(jnp.bfloat16), 'tensor', scatter_dime...  53.6 us
  transfers between devices with their start and end apart: 43, of which 31 were waited for; matrix products, arithmetic and copies ran while one was open for 13% of the time, Pallas kernels for 0%

commit v1 on v0

v1 whole, which is shorter than its diff:
```python
import jax
import jax.numpy as jnp
from jax import lax
from jax.sharding import PartitionSpec as P

HEAD_DIM = 64
NORM_EPS = 1e-12
MASKED = -1000000000.0
ROOT_HALF = 0.7071067811865476
INV_ROOT_TWOPI = 0.3989422804014327
LOW = jnp.bfloat16


def swapped(block, axis, bit):
    size = lax.axis_size(axis)
    return lax.ppermute(block, axis, [(i, i ^ bit) for i in range(size)])


def halve_sum(stack, axis, dim, kind):
    size = lax.axis_size(axis)
    own = lax.axis_index(axis)
    bit = 1
    while bit < size:
        count = stack.shape[dim]
        split = stack.reshape(stack.shape[:dim] + (count // 2, 2) + stack.shape[dim + 1 :])
        side = (own // bit) % 2
        kept = lax.dynamic_index_in_dim(split, side, dim + 1, keepdims=False)
        given = lax.dynamic_index_in_dim(split, 1 - side, dim + 1, keepdims=False)
        came = swapped(given, axis, bit)
        stack = (kept.astype(jnp.float32) + came.astype(jnp.float32)).astype(kind)
        bit *= 2
    return lax.squeeze(stack, (dim,))


def dot_rows(left_side, right_side):
    return lax.dot_general(
        left_side, right_side, (((0,), (0,)), ((), ())), preferred_element_type=jnp.float32
    )


def dot_cols(left_side, right_side):
    return lax.dot_general(
        left_side, right_side, (((1,), (1,)), ((), ())), preferred_element_type=jnp.float32
    )


def dot(left_side, right_side):
    return jnp.dot(left_side, right_side, preferred_element_type=jnp.float32)


def gather_tokens(rows):
    return lax.all_gather(rows, "tensor", axis=0, tiled=True)


def scatter_tokens(partial):
    return lax.psum_scatter(
        partial.astype(LOW), "tensor", scatter_dimension=0, tiled=True
    ).astype(jnp.float32)


def norm_forward(values, gain_row, shift_row):
    center = values - jnp.mean(values, axis=-1, keepdims=True)
    spread = jnp.mean(center * center, axis=-1, keepdims=True)
    inverse = lax.rsqrt(spread + NORM_EPS)
    scaled = center * inverse
    return (scaled * gain_row + shift_row, scaled, inverse)


def norm_backward(upstream, scaled, inverse, gain_row):
    weighted = upstream * gain_row
    inner_term = (
        weighted
        - jnp.mean(weighted, axis=-1, keepdims=True)
        - scaled * jnp.mean(weighted * scaled, axis=-1, keepdims=True)
    )
    return (inverse * inner_term, jnp.sum(upstream * scaled, axis=0), jnp.sum(upstream, axis=0))


def gelu_slope(values):
    return 0.5 * (1.0 + lax.erf(values * ROOT_HALF)) + values * INV_ROOT_TWOPI * jnp.exp(
        -0.5 * values * values
    )


def to_heads(rows, micro):
    parts = lax.axis_size("tensor")
    width = rows.shape[-1]
    shaped = rows.reshape(parts, micro, -1, width // HEAD_DIM, HEAD_DIM)
    shaped = shaped.transpose(1, 3, 0, 2, 4)
    return shaped.reshape(micro, width // HEAD_DIM, -1, HEAD_DIM)


def from_heads(block):
    micro, heads, count, _ = block.shape
    parts = lax.axis_size("tensor")
    shaped = block.reshape(micro, heads, parts, count // parts, HEAD_DIM)
    return shaped.transpose(2, 0, 3, 1, 4).reshape(micro * count, heads * HEAD_DIM)


def attend(queries, key_rows, value_rows, allowed):
    scores = jnp.einsum(
        "mhqe,mhke->mhqk", queries, key_rows, preferred_element_type=jnp.float32
    ) * HEAD_DIM ** (-0.5)
    scores = jnp.where(allowed, scores, MASKED)
    largest = jnp.max(scores, axis=-1, keepdims=True)
    raised = jnp.exp(scores - largest)
    probs = raised / jnp.sum(raised, axis=-1, keepdims=True)
    context = jnp.einsum(
        "mhqk,mhke->mhqe", probs.astype(LOW), value_rows, preferred_element_type=jnp.float32
    )
    return (context.astype(LOW), probs)


def attend_back(queries, key_rows, value_rows, probs, grad_context):
    scale = HEAD_DIM ** (-0.5)
    grad_probs = jnp.einsum(
        "mhqe,mhke->mhqk", grad_context, value_rows, preferred_element_type=jnp.float32
    )
    inner_term = jnp.sum(probs * grad_probs, axis=-1, keepdims=True)
    grad_scores = (probs * (grad_probs - inner_term)).astype(LOW)
    grad_query = (
        jnp.einsum("mhqk,mhke->mhqe", grad_scores, key_rows, preferred_element_type=jnp.float32)
        * scale
    )
    grad_keys = (
        jnp.einsum("mhqk,mhqe->mhke", grad_scores, queries, preferred_element_type=jnp.float32)
        * scale
    )
    grad_values = jnp.einsum(
        "mhqk,mhqe->mhke", probs.astype(LOW), grad_context, preferred_element_type=jnp.float32
    )
    return [from_heads(member.astype(LOW)) for member in (grad_query, grad_keys, grad_values)]


def layer_forward(current, micro, allowed, weights, vectors):
    w_qkv, w_o, w_in, w_out = weights
    gains, biases, query_bias, value_bias, local_hidden_bias = vectors
    gathered = gather_tokens(current)
    width = query_bias.shape[0]
    projected = dot(gathered, w_qkv)
    queries = to_heads((projected[:, :width] + query_bias).astype(LOW), micro)
    key_rows = to_heads(projected[:, width : 2 * width].astype(LOW), micro)
    value_rows = to_heads((projected[:, 2 * width :] + value_bias).astype(LOW), micro)
    context, probs = attend(queries, key_rows, value_rows, allowed)
    context = from_heads(context)
    mixed_rows = scatter_tokens(dot(context, w_o))
    normed, scaled_one, inverse_one = norm_forward(
        current.astype(jnp.float32) + mixed_rows + biases[2], gains[0], biases[3]
    )
    spread_rows = gather_tokens(normed.astype(LOW))
    hidden = dot(spread_rows, w_in) + local_hidden_bias
    active = jax.nn.gelu(hidden, approximate=False).astype(LOW)
    branch = scatter_tokens(dot(active, w_out))
    final_rows, scaled_two, inverse_two = norm_forward(
        normed + branch + biases[4], gains[1], biases[5]
    )
    kept = (
        gathered, queries, key_rows, value_rows, probs, context, scaled_one, inverse_one,
        spread_rows, hidden, active, scaled_two, inverse_two,
    )
    return (final_rows.astype(LOW), kept)


def layer_backward(upstream, kept, weights, gains):
    (
        gathered, queries, key_rows, value_rows, probs, context, scaled_one, inverse_one,
        spread_rows, hidden, active, scaled_two, inverse_two,
    ) = kept
    micro = queries.shape[0]
    w_qkv, w_o, w_in, w_out = weights
    grad_second, gain_two, shift_two = norm_backward(upstream, scaled_two, inverse_two, gains[1])
    grad_feed = gather_tokens(grad_second.astype(LOW))
    grad_active = dot_cols(grad_feed, w_out)
    grad_hidden = (grad_active * gelu_slope(hidden)).astype(LOW)
    part = scatter_tokens(dot_cols(grad_hidden, w_in))
    grad_w_out = dot_rows(active, grad_feed).astype(LOW)
    grad_w_in = dot_rows(spread_rows, grad_hidden).astype(LOW)
    grad_normed = grad_second + part
    grad_first, gain_one, shift_one = norm_backward(grad_normed, scaled_one, inverse_one, gains[0])
    grad_mix = gather_tokens(grad_first.astype(LOW))
    grad_context = to_heads(dot_cols(grad_mix, w_o).astype(LOW), micro)
    pieces = attend_back(queries, key_rows, value_rows, probs, grad_context)
    grad_project = jnp.concatenate(pieces, axis=1)
    part = scatter_tokens(dot_cols(grad_project, w_qkv))
    grad_w_o = dot_rows(context, grad_mix).astype(LOW)
    grad_w_qkv = dot_rows(gathered, grad_project).astype(LOW)
    grad_current = grad_first + part
    width = pieces[0].shape[1]
    column_sums = jnp.sum(grad_project.astype(jnp.float32), axis=0)
    row_grads = jnp.stack(
        [
            gain_one, gain_two, jnp.sum(grad_first, axis=0), shift_one,
            jnp.sum(grad_second, axis=0), shift_two,
        ]
    )
    hidden_grads = jnp.sum(grad_hidden.astype(jnp.float32), axis=0)
    return (
        grad_current.astype(LOW),
        (grad_w_qkv, grad_w_o, grad_w_in, grad_w_out),
        (row_grads, column_sums[:width], column_sums[2 * width :], hidden_grads),
    )


def body(inputs, segments, cotangent, w_qkv, w_o, w_in, w_out, ln_gains, model_biases, hidden_bias):
    half = lax.axis_index("pipe")
    first = half == 0
    column = lax.axis_index("tensor")
    sections = lax.axis_size("pipe")
    parts = lax.axis_size("dp")
    columns = lax.axis_size("tensor")
    micro = inputs.shape[0] // sections
    row_count = inputs.shape[1]
    model_width = inputs.shape[2]
    width = w_qkv.shape[-1]
    hidden_local = w_in.shape[-1]
    hidden_width = hidden_bias.shape[-1]
    block = w_qkv.shape[1]

    shards = (
        w_qkv[0].reshape(block, 3 * width), w_o[0].T, w_in[0], w_out[0].T
    )
    stacks = [
        lax.all_gather(shard, ("pipe", "dp"), axis=0, tiled=True).reshape(
            sections, parts * shard.shape[0], shard.shape[1]
        )
        for shard in shards
    ]
    gains_all = lax.all_gather(ln_gains[0], "pipe")
    biases_all = lax.all_gather(model_biases[0], "pipe")
    hidden_all = lax.all_gather(hidden_bias[0], "pipe")

    def own_slice(array, size, dim):
        return lax.dynamic_slice_in_dim(array, column * size, size, dim)

    def own_micro(array):
        return lax.dynamic_slice_in_dim(array, half * micro, micro, 0)

    labels = own_micro(segments)
    allowed = (labels[:, :, None] == labels[:, None, :])[:, None]
    weights, vectors = [], []
    for layer in range(sections):
        weights.append(
            (stacks[0][layer], stacks[1][layer].T, stacks[2][layer], stacks[3][layer].T)
        )
        biases = biases_all[layer]
        vectors.append(
            (
                gains_all[layer], biases, own_slice(biases[0], width, 0),
                own_slice(biases[1], width, 0), own_slice(hidden_all[layer], hidden_local, 0),
            )
        )
    current = own_micro(inputs).reshape(micro * row_count, model_width)
    outs, kept_list = [], []
    for layer in range(sections):
        current, kept = layer_forward(current, micro, allowed, weights[layer], vectors[layer])
        outs.append(current)
        kept_list.append(kept)
    upstream = own_micro(cotangent).reshape(micro * row_count, model_width)
    grads = [None] * sections
    totals = [None] * sections
    packs = [None] * sections
    zero = jnp.zeros((), jnp.int32)
    for layer in reversed(range(sections)):
        upstream, weight_grads, vector_grads = layer_backward(
            upstream.astype(jnp.float32), kept_list[layer], weights[layer], vectors[layer][0]
        )
        grads[layer] = upstream
        shaped = (
            weight_grads[0].reshape(parts, block, 3 * width),
            weight_grads[1].reshape(width, parts, model_width // parts),
            weight_grads[2].reshape(parts, block, hidden_local),
            weight_grads[3].reshape(hidden_local, parts, model_width // parts),
        )
        totals[layer] = [
            halve_sum(member, "dp", dim, LOW) for member, dim in zip(shaped, (0, 1, 0, 1))
        ]
        row_grads, query_grad, value_grad, hidden_grads = vector_grads
        placed = lax.dynamic_update_slice(
            jnp.zeros((2, model_width), jnp.float32),
            jnp.stack([query_grad, value_grad]),
            (zero, column * width),
        )
        hidden_full = lax.dynamic_update_slice(
            jnp.zeros((hidden_width,), jnp.float32), hidden_grads, (column * hidden_local,)
        )
        blocks = parts * columns
        packs[layer] = jnp.concatenate(
            [
                jnp.concatenate([row_grads[:2], placed, row_grads[2:]], axis=0)
                .reshape(8, blocks, model_width // blocks)
                .transpose(1, 0, 2)
                .reshape(blocks, -1),
                hidden_full.reshape(blocks, hidden_width // blocks),
            ],
            axis=1,
        )

    def exchanged(pair):
        return jnp.where(first, pair[0], pair[1]), swapped(jnp.where(first, pair[1], pair[0]), "pipe", 1)

    summed = []
    for index in range(4):
        own, came = exchanged([totals[0][index], totals[1][index]])
        summed.append(own.astype(jnp.float32) + came.astype(jnp.float32))
    own, came = exchanged(packs)
    pack = (own + came).reshape(parts, columns, -1)
    pack = halve_sum(pack, "dp", 0, jnp.float32)
    pack = halve_sum(pack, "tensor", 0, jnp.float32)
    rows_each = model_width // (parts * columns)
    vector_part = pack[: 8 * rows_each].reshape(8, rows_each)

    def both_halves(pair):
        own, came = exchanged(pair)
        shape = (micro, row_count, model_width)
        own, came = own.reshape(shape), came.reshape(shape)
        return jnp.concatenate(
            [jnp.where(first, own, came), jnp.where(first, came, own)], axis=0
        )[None]

    return (
        both_halves(outs),
        both_halves(grads),
        summed[0].reshape(1, block, 3, width),
        summed[1][None],
        summed[2][None],
        summed[3][None],
        vector_part[:2][None],
        vector_part[2:][None],
        pack[8 * rows_each :][None],
    )


def solution(mesh):
    return jax.shard_map(
        body,
        mesh=mesh,
        in_specs=(
            P(None, ("dp", "tensor"), None),
            P(None, "dp"),
            P(None, ("dp", "tensor"), None),
            P("pipe", "dp", None, "tensor"),
            P("pipe", "tensor", "dp"),
            P("pipe", "dp", "tensor"),
            P("pipe", "tensor", "dp"),
            P("pipe", None, None),
            P("pipe", None, None),
            P("pipe", None),
        ),
        out_specs=(
            P("pipe", None, ("dp", "tensor"), None),
            P("pipe", None, ("dp", "tensor"), None),
            P("pipe", "dp", None, "tensor"),
            P("pipe", "tensor", "dp"),
            P("pipe", "dp", "tensor"),
            P("pipe", "tensor", "dp"),
            P("pipe", None, ("dp", "tensor")),
            P("pipe", None, ("dp", "tensor")),
            P("pipe", ("dp", "tensor")),
        ),
        check_vma=False,
    )
```

time: 1340 us -> 761 us (0.57)
  blocking collectives: 467 us -> 14.3 us
  matrix products: 163 us -> 91.5 us
  other arithmetic: 113 us -> 62.2 us
  local copies, waits for them, and re-layouts: 58.1 us -> 106 us
  waiting for transfers between devices: 478 us -> 437 us
    all_gather x25 -> x3, blocking collectives: 409 us -> 14.3 us  [the longest x1 5.51 us: body(): biases_all = lax.all_gather(model_biases[0], 'pipe')]
    reduce_scatter x28 -> x8, waiting for transfers between devices: 425 us -> 138 us  [scatter_tokens(): lax.psum_scatter(partial.astype(LOW), 'tensor', scatter_dimension=0, tile...]
    all_gather x3 -> x12, waiting for transfers between devices: 22.2 us -> 275 us  [the longest x8 168 us: gather_tokens(): return lax.all_gather(rows, 'tensor', axis=0, tiled=True)]
    unnamed x1 -> x0, blocking collectives: 57.9 us -> none
    dot_general x76 -> x18, matrix products: 96.6 us -> 44.8 us  [the longest x8 32 us: dot(): return jnp.dot(left_side, right_side, preferred_element_type=jnp.float32)]
    reshape x0 -> x44, local copies, waits for them, and re-layouts: none -> 30.3 us  [the longest x16 15.3 us: from_heads(): shaped = block.reshape(micro, heads, parts, count // parts, HEAD_DIM)]
    dot_general x18 -> x8, matrix products: 39.3 us -> 17.8 us  [dot_rows(): lax.dot_general(left_side, right_side, (((0,), (0,)), ((), ())), preferre...]
    dynamic_slice x3 -> x19, local copies, waits for them, and re-layouts: 0.05 us -> 20.7 us  [the longest x6 10.7 us: halve_sum(): given = lax.dynamic_index_in_dim(split, 1 - side, dim + 1, keepdims=False)]
  transfers between devices with their start and end apart: 43 -> 47, of which waited for: 31 -> 24; matrix products, arithmetic and copies ran while one was open for 13% -> 26% of each run, Pallas kernels for 0% -> 0%
where the time goes in v1:
time: 761 us; the launch traced here: 750 us
  waiting for transfers between devices  437 us (57%)
  local copies, waits for them, and re-layouts  106 us (14%)
  matrix products  91.5 us (12%)
  other arithmetic  62.2 us (8%)
  starting transfers between devices  22.5 us (3%)
  between operations  16.3 us (2%)
  blocking collectives  14.3 us (2%)
    all_gather x8, waiting for transfers between devices, gather_tokens(): return lax.all_gather(rows, 'tensor', axis=0, tiled=True)  168 us
    reduce_scatter x8, waiting for transfers between devices, scatter_tokens(): lax.psum_scatter(partial.astype(LOW), 'tensor', scatter_dimension=0, tile...  138 us
    all_gather x4, waiting for transfers between devices, body(): lax.all_gather(shard, ('pipe', 'dp'), axis=0, tiled=True)  107 us
    dot_general x8, matrix products, dot(): return jnp.dot(left_side, right_side, preferred_element_type=jnp.float32)  32 us
    unnamed x178, local copies, waits for them, and re-layouts  27 us
    dot_general x8, matrix products, dot_cols(): lax.dot_general(left_side, right_side, (((1,), (1,)), ((), ())), preferre...  25.1 us
    ppermute x27, waiting for transfers between devices, swapped(): return lax.ppermute(block, axis, [(i, i ^ bit) for i in range(size)])  21.4 us
    ppermute x27, starting transfers between devices, swapped(): return lax.ppermute(block, axis, [(i, i ^ bit) for i in range(size)])  20.4 us
  transfers between devices with their start and end apart: 47, of which 24 were waited for; matrix products, arithmetic and copies ran while one was open for 26% of the time, Pallas kernels for 0%

profile of v1, /device:TPU:0, one launch (start us, length us, event | category | flops | bytes accessed | tf_op | source)
XLA Modules:
  0.0 750.4 jit_solution(10299277571074806249)
XLA Ops:
  11.8 5.5 all_gather.47
  18.2 22.7 %all-gather.15.cloned.1.call-done = bf16[512,1024]{1,0:T(8,128)(2,1)} async-done(((bf16[128,1024]{1,0:T(8,128)(2,1)}), bf16[512,1024]{1,0:T(8,128)(2,1)}) %all-gather.15.cloned.1.call-update) | async-done | bytes 1048592 | tf_op jit(solution)/shard_map/all_gather | solution.py:52
  40.9 34.6 %all-gather.17.cloned.1.call-done = bf16[2048,768]{0,1:T(8,128)(2,1)} async-done(((bf16[256,768]{0,1:T(8,128)(2,1)}), bf16[2048,768]{0,1:T(8,128)(2,1)}) %all-gather.17.cloned.1.call-update) | async-done | bytes 3145744 | tf_op jit(solution)/shard_map/all_gather | solution.py:223
  75.5 2.7 fusion.64
  86.3 14.6 %all-gather.19.cloned.1.call-done = bf16[2048,256]{0,1:T(8,128)(2,1)} async-done(((bf16[256,256]{0,1:T(8,128)(2,1)}), bf16[2048,256]{0,1:T(8,128)(2,1)}) %all-gather.19.cloned.1.call-update) | async-done | bytes 1048592 | tf_op jit(solution)/shard_map/all_gather | solution.py:223
  100.9 2.5 convolution_convert_fusion.9
  104.0 4.4 all_gather.49
  108.4 22.5 %reduce-scatter.9.cloned.1.call-done = bf16[128,1024]{1,0:T(8,128)(2,1)} async-done(((bf16[512,1024]{1,0:T(8,128)(2,1)}), bf16[128,1024]{1,0:T(8,128)(2,1)}) %reduce-scatter.9.cloned.1.call-update) | async-done | bytes 262160 | tf_op jit(solution)/shard_map/reduce_scatter | solution.py:56
  135.9 4.4 all-gather.1
  140.3 27.5 %all-gather.37.cloned.1.call-done = bf16[1,2048,1024]{2,1,0:T(8,128)(2,1)} async-done(((bf16[1,256,1024]{2,1,0:T(8,128)(2,1)}), bf16[1,2048,1024]{2,1,0:T(8,128)(2,1)}) %all-gather.37.cloned.1.call-update) | async-done | bytes 4194320 | tf_op jit(solution)/shard_map/all_gather | solution.py:223
  167.8 30.0 %all-gather.21.cloned.1.call-done = bf16[512,1024]{1,0:T(8,128)(2,1)} async-done(((bf16[128,1024]{1,0:T(8,128)(2,1)}), bf16[512,1024]{1,0:T(8,128)(2,1)}) %all-gather.21.cloned.1.call-update) | async-done | bytes 1048592 | tf_op jit(solution)/shard_map/all_gather | solution.py:52
  197.8 8.2 %fusion.4 = (bf16[512,1024]{1,0:T(8,128)(2,1)S(1)}, f32[512,1024]{1,0:T(8,128)}) fusion(f32[1024]{0:T(1024)S(1)} %bitcast.387, bf16[512,1024]{1,0:T(8,128)(2,1)} %all-gather.21.cloned.1.call-done, bf16[1,2048,1024]{2,1,0:T(8,128)(2,1)} %all-gather.37.cloned.1.call-done), kind=kOutput, calls=%fused_computation.8 | convolution fusion | flops 1108344832 | bytes 6295552 | tf_op jit(solution)/shard_map/dot_general | solution.py:48
  206.0 30.4 %all-gather.23.cloned.1.call-done = bf16[2048,1024]{0,1:T(8,128)(2,1)} async-done(((bf16[256,1024]{0,1:T(8,128)(2,1)}), bf16[2048,1024]{0,1:T(8,128)(2,1)}) %all-gather.23.cloned.1.call-update) | async-done | bytes 4194320 | tf_op jit(solution)/shard_map/all_gather | solution.py:223
  236.4 3.9 fusion.52
  240.4 27.4 %reduce-scatter.11.cloned.1.call-done = bf16[128,1024]{1,0:T(8,128)(2,1)} async-done(((bf16[512,1024]{1,0:T(8,128)(2,1)}), bf16[128,1024]{1,0:T(8,128)(2,1)}) %reduce-scatter.11.cloned.1.call-update) | async-done | bytes 262160 | tf_op jit(solution)/shard_map/reduce_scatter | solution.py:56
  270.4 26.4 %all-gather.25.cloned.1.call-done = bf16[512,1024]{1,0:T(8,128)(2,1)} async-done(((bf16[128,1024]{1,0:T(8,128)(2,1)}), bf16[512,1024]{1,0:T(8,128)(2,1)}) %all-gather.25.cloned.1.call-update) | async-done | bytes 1048592 | tf_op jit(solution)/shard_map/all_gather | solution.py:52
  296.8 2.7 fusion.61
  314.0 26.8 %reduce-scatter.13.cloned.1.call-done = bf16[128,1024]{1,0:T(8,128)(2,1)} async-done(((bf16[512,1024]{1,0:T(8,128)(2,1)}), bf16[128,1024]{1,0:T(8,128)(2,1)}) %reduce-scatter.13.cloned.1.call-update) | async-done | bytes 262160 | tf_op jit(solution)/shard_map/reduce_scatter | solution.py:56
  345.4 26.5 %all-gather.27.cloned.1.call-done = bf16[512,1024]{1,0:T(8,128)(2,1)} async-done(((bf16[128,1024]{1,0:T(8,128)(2,1)}), bf16[512,1024]{1,0:T(8,128)(2,1)}) %all-gather.27.cloned.1.call-update) | async-done | bytes 1048592 | tf_op jit(solution)/shard_map/all_gather | solution.py:52
  372.0 8.3 %fusion.7 = (bf16[512,1024]{1,0:T(8,128)(2,1)S(1)}, f32[512,1024]{1,0:T(8,128)}) fusion(f32[1024]{0:T(1024)S(1)} %bitcast.389, bf16[512,1024]{1,0:T(8,128)(2,1)} %all-gather.27.cloned.1.call-done, bf16[1,2048,1024]{2,1,0:T(8,128)(2,1)} %all-gather.37.cloned.1.call-done), kind=kOutput, calls=%fused_computation.11 | convolution fusion | flops 1108344832 | bytes 6295552 | tf_op jit(solution)/shard_map/dot_general | solution.py:48
  383.9 26.5 %reduce-scatter.15.cloned.1.call-done = bf16[128,1024]{1,0:T(8,128)(2,1)} async-done(((bf16[512,1024]{1,0:T(8,128)(2,1)}), bf16[128,1024]{1,0:T(8,128)(2,1)}) %reduce-scatter.15.cloned.1.call-update) | async-done | bytes 262160 | tf_op jit(solution)/shard_map/reduce_scatter | solution.py:56
  413.7 26.2 %all-gather.29.cloned.1.call-done = bf16[512,1024]{1,0:T(8,128)(2,1)} async-done(((bf16[128,1024]{1,0:T(8,128)(2,1)}), bf16[512,1024]{1,0:T(8,128)(2,1)}) %all-gather.29.cloned.1.call-update) | async-done | bytes 1048592 | tf_op jit(solution)/shard_map/all_gather | solution.py:52
  439.9 4.6 convert_reduce_fusion
  447.8 26.8 %reduce-scatter.17.cloned.1.call-done = bf16[128,1024]{1,0:T(8,128)(2,1)} async-done(((bf16[512,1024]{1,0:T(8,128)(2,1)}), bf16[128,1024]{1,0:T(8,128)(2,1)}) %reduce-scatter.17.cloned.1.call-update) | async-done | bytes 262160 | tf_op jit(solution)/shard_map/reduce_scatter | solution.py:56
  480.8 2.8 convolution_convert_fusion.2
  486.0 18.8 %all-gather.31.cloned.1.call-done = bf16[512,1024]{1,0:T(8,128)(2,1)} async-done(((bf16[128,1024]{1,0:T(8,128)(2,1)}), bf16[512,1024]{1,0:T(8,128)(2,1)}) %all-gather.31.cloned.1.call-update) | async-done | bytes 1048592 | tf_op jit(solution)/shard_map/all_gather | solution.py:52
  507.7 2.9 convolution_convert_fusion.16
  517.4 3.6 convolution_convert_fusion.7
  521.3 2.8 convolution_convert_fusion
  525.3 2.3 copy.167
  539.7 8.2 %reduce-scatter.19.cloned.1.call-done = bf16[128,1024]{1,0:T(8,128)(2,1)} async-done(((bf16[512,1024]{1,0:T(8,128)(2,1)}), bf16[128,1024]{1,0:T(8,128)(2,1)}) %reduce-scatter.19.cloned.1.call-update) | async-done | bytes 262160 | tf_op jit(solution)/shard_map/reduce_scatter | solution.py:56
  555.4 2.5 convolution_convert_fusion.4
  559.2 17.7 %all-gather.33.cloned.1.call-done = bf16[512,1024]{1,0:T(8,128)(2,1)} async-done(((bf16[128,1024]{1,0:T(8,128)(2,1)}), bf16[512,1024]{1,0:T(8,128)(2,1)}) %all-gather.33.cloned.1.call-update) | async-done | bytes 1048592 | tf_op jit(solution)/shard_map/all_gather | solution.py:52
  577.0 5.2 convert_reduce_fusion.1
  585.7 2.5 convolution_convert_fusion.3
  593.4 2.3 copy.165
  595.8 2.3 copy.182
  598.1 2.3 copy.157
  621.8 3.4 collective-permute-done.13
  648.0 3.1 fusion.75
  654.1 2.9 convolution_convert_fusion.14
  686.3 3.6 convolution_convert_fusion.6
  690.6 3.6 convolution_convert_fusion.5
  695.9 2.7 constant_dynamic-slice_fusion.26
  698.6 2.3 copy.155
  702.6 2.5 fusion.74
  716.9 6.2 collective-permute-done.3
  730.7 6.8 collective-permute-done.6
  (487 shorter events, 204.5 us)
Async XLA Ops:
  7.2 33.7 %all-gather.15.cloned.1.call-start = ((), (), s32[]{:S(2)}) async-start(), calls=%async_computation.8 | async-start | bytes 1310720 | tf_op jit(solution)/shard_map/all_gather | solution.py:52
  9.0 66.5 %all-gather.17.cloned.1.call-start = ((), (), s32[]{:S(2)}) async-start(), calls=%async_computation.9 | async-start | bytes 3538944 | tf_op jit(solution)/shard_map/all_gather | solution.py:223
  11.0 89.9 %all-gather.19.cloned.1.call-start = ((), (), s32[]{:S(2)}) async-start(), calls=%async_computation.10 | async-start | bytes 1179648 | tf_op jit(solution)/shard_map/all_gather | solution.py:223
  11.7 119.2 %reduce-scatter.9.cloned.1.call-start = ((), (), s32[]{:S(2)}) async-start(), calls=%async_computation.11 | async-start | bytes 1310720 | tf_op jit(solution)/shard_map/reduce_scatter | solution.py:56
  103.4 64.4 %all-gather.37.cloned.1.call-start = ((), (), s32[]{:S(2)}) async-start(), calls=%async_computation.27 | async-start | bytes 4718592 | tf_op jit(solution)/shard_map/all_gather | solution.py:223
  104.0 93.8 %all-gather.21.cloned.1.call-start = ((), (), s32[]{:S(2)}) async-start(), calls=%async_computation.12 | async-start | bytes 1310720 | tf_op jit(solution)/shard_map/all_gather | solution.py:52
  132.1 135.7 %copy-start.57 = (f32[128]{0:T(128)}, f32[128]{0:T(128)S(1)}, u32[]{:S(2)}) copy-start(f32[128]{0:T(128)S(1)} %broadcast_multiply_fusion.11) | copy-start | bytes 1540
  135.1 101.3 %all-gather.23.cloned.1.call-start = ((), (), s32[]{:S(2)}) async-start(), calls=%async_computation.13 | async-start | bytes 4718592 | tf_op jit(solution)/shard_map/all_gather | solution.py:223
  135.8 131.9 %reduce-scatter.11.cloned.1.call-start = ((), (), s32[]{:S(2)}) async-start(), calls=%async_computation.14 | async-start | bytes 1310720 | tf_op jit(solution)/shard_map/reduce_scatter | solution.py:56
  240.3 56.5 %all-gather.25.cloned.1.call-start = ((), (), s32[]{:S(2)}) async-start(), calls=%async_computation.15 | async-start | bytes 1310720 | tf_op jit(solution)/shard_map/all_gather | solution.py:52
  270.2 70.7 %reduce-scatter.13.cloned.1.call-start = ((), (), s32[]{:S(2)}) async-start(), calls=%async_computation.16 | async-start | bytes 1310720 | tf_op jit(solution)/shard_map/reduce_scatter | solution.py:56
  314.0 58.0 %all-gather.27.cloned.1.call-start = ((), (), s32[]{:S(2)}) async-start(), calls=%async_computation.17 | async-start | bytes 1310720 | tf_op jit(solution)/shard_map/all_gather | solution.py:52
  345.4 65.0 %reduce-scatter.15.cloned.1.call-start = ((), (), s32[]{:S(2)}) async-start(), calls=%async_computation.18 | async-start | bytes 1310720 | tf_op jit(solution)/shard_map/reduce_scatter | solution.py:56
  383.5 56.4 %all-gather.29.cloned.1.call-start = ((), (), s32[]{:S(2)}) async-start(), calls=%async_computation.19 | async-start | bytes 1310720 | tf_op jit(solution)/shard_map/all_gather | solution.py:52
  413.3 61.3 %reduce-scatter.17.cloned.1.call-start = ((), (), s32[]{:S(2)}) async-start(), calls=%async_computation.20 | async-start | bytes 1310720 | tf_op jit(solution)/shard_map/reduce_scatter | solution.py:56
  447.8 57.0 %all-gather.31.cloned.1.call-start = ((), (), s32[]{:S(2)}) async-start(), calls=%async_computation.21 | async-start | bytes 1310720 | tf_op jit(solution)/shard_map/all_gather | solution.py:52
  478.2 69.8 %reduce-scatter.19.cloned.1.call-start = ((), (), s32[]{:S(2)}) async-start(), calls=%async_computation.22 | async-start | bytes 1310720 | tf_op jit(solution)/shard_map/reduce_scatter | solution.py:56
  479.3 48.5 %collective-permute-start = (bf16[128,1024]{1,0:T(8,128)(2,1)}, bf16[128,1024]{1,0:T(8,128)(2,1)}, u32[]{:S(2)}, u32[]{:S(2)}) collective-permute-start(bf16[128,1024]{1,0:T(8,128)(2,1)} %get-tuple-element.65), channel_id=1, source_target_pairs={{0,16},{16,0},{1,17},{17,1},{2,18},{18,2},{3,19},{19,3},{4,20},{20... | collective-permute-start | bytes 786440 | tf_op jit(solution)/shard_map/ppermute | solution.py:16
  486.0 46.1 %collective-permute-start.14 = (bf16[2,256,1024]{2,1,0:T(8,128)(2,1)}, bf16[2,256,1024]{2,1,0:T(8,128)(2,1)}, u32[]{:S(2)}, u32[]{:S(2)}) collective-permute-start(bf16[2,256,1024]{2,1,0:T(8,128)(2,1)} %dynamic-slice_bitcast_fusion), channel_id=1, source_target_pairs={{0,4},{4,0},{8,12},{12,8},{1,5},{5,1},{9,13},{13,9},{2,6},{6,2},{1... | collective-permute-start | bytes 3145736 | tf_op jit(solution)/shard_map/ppermute | solution.py:16
  521.1 55.8 %all-gather.33.cloned.1.call-start = ((), (), s32[]{:S(2)}) async-start(), calls=%async_computation.23 | async-start | bytes 1310720 | tf_op jit(solution)/shard_map/all_gather | solution.py:52
  527.7 8.8 %collective-permute-start.19 = (bf16[1024,2,256]{2,0,1:T(8,128)(2,1)}, bf16[1024,2,256]{2,0,1:T(8,128)(2,1)}, u32[]{:S(2)}, u32[]{:S(2)}) collective-permute-start(bf16[1024,2,256]{2,0,1:T(8,128)(2,1)} %bitcast.319), channel_id=1, source_target_pairs={{0,4},{4,0},{8,12},{12,8},{1,5},{5,1},{9,13},{13,9},{2,6},{6,2},{1... | collective-permute-start | bytes 3145736 | tf_op jit(solution)/shard_map/ppermute | solution.py:16
  535.0 86.8 %collective-permute-start.15 = (bf16[1,256,1024]{2,1,0:T(8,128)(2,1)}, bf16[1,256,1024]{2,1,0:T(8,128)(2,1)}, u32[]{:S(2)}, u32[]{:S(2)}) collective-permute-start(bf16[1,256,1024]{2,1,0:T(8,128)(2,1)} %constant_dynamic-slice_fusion.13), channel_id=1, source_target_pairs={{0,8},{4,12},{8,0},{12,4},{1,9},{5,13},{9,1},{13,5},{2,10},{6,14},... | collective-permute-start | bytes 1572872 | tf_op jit(solution)/shard_map/ppermute | solution.py:16
  538.9 95.2 %collective-permute-start.20 = (bf16[1024,1,256]{2,0,1:T(8,128)(2,1)}, bf16[1024,1,256]{2,0,1:T(8,128)(2,1)}, u32[]{:S(2)}, u32[]{:S(2)}) collective-permute-start(bf16[1024,1,256]{2,0,1:T(8,128)(2,1)} %constant_dynamic-slice_fusion.7), channel_id=1, source_target_pairs={{0,8},{4,12},{8,0},{12,4},{1,9},{5,13},{9,1},{13,5},{2,10},{6,14},... | collective-permute-start | bytes 1572872 | tf_op jit(solution)/shard_map/ppermute | solution.py:16
  550.3 61.9 %reduce-scatter.21.cloned.1.call-start = ((), (), s32[]{:S(2)}) async-start(), calls=%async_computation.24 | async-start | bytes 1310720 | tf_op jit(solution)/shard_map/reduce_scatter | solution.py:56
  555.1 46.0 %collective-permute-start.9 = (bf16[256,2,256]{2,0,1:T(8,128)(2,1)}, bf16[256,2,256]{2,0,1:T(8,128)(2,1)}, u32[]{:S(2)}, u32[]{:S(2)}) collective-permute-start(bf16[256,2,256]{2,0,1:T(8,128)(2,1)} %bitcast.289), channel_id=1, source_target_pairs={{0,4},{4,0},{8,12},{12,8},{1,5},{5,1},{9,13},{13,9},{2,6},{6,2},{1... | collective-permute-start | bytes 786440 | tf_op jit(solution)/shard_map/ppermute | solution.py:16
  585.4 65.7 %all-gather.35.cloned.1.call-start = ((), (), s32[]{:S(2)}) async-start(), calls=%async_computation.25 | async-start | bytes 1310720 | tf_op jit(solution)/shard_map/all_gather | solution.py:52
  589.9 15.6 %collective-permute-start.12 = (bf16[2,256,1024]{2,1,0:T(8,128)(2,1)}, bf16[2,256,1024]{2,1,0:T(8,128)(2,1)}, u32[]{:S(2)}, u32[]{:S(2)}) collective-permute-start(bf16[2,256,1024]{2,1,0:T(8,128)(2,1)} %dynamic-slice_bitcast_fusion.1), channel_id=1, source_target_pairs={{0,4},{4,0},{8,12},{12,8},{1,5},{5,1},{9,13},{13,9},{2,6},{6,2},{1... | collective-permute-start | bytes 3145736 | tf_op jit(solution)/shard_map/ppermute | solution.py:16
  595.6 14.1 %collective-permute-start.17 = (bf16[1024,2,256]{2,0,1:T(8,128)(2,1)}, bf16[1024,2,256]{2,0,1:T(8,128)(2,1)}, u32[]{:S(2)}, u32[]{:S(2)}) collective-permute-start(bf16[1024,2,256]{2,0,1:T(8,128)(2,1)} %bitcast.320), channel_id=1, source_target_pairs={{0,4},{4,0},{8,12},{12,8},{1,5},{5,1},{9,13},{13,9},{2,6},{6,2},{1... | collective-permute-start | bytes 3145736 | tf_op jit(solution)/shard_map/ppermute | solution.py:16
  601.1 17.6 %collective-permute-start.4 = (bf16[2,256,768]{1,2,0:T(8,128)(2,1)}, bf16[2,256,768]{1,2,0:T(8,128)(2,1)}, u32[]{:S(2)}, u32[]{:S(2)}) collective-permute-start(bf16[2,256,768]{1,2,0:T(8,128)(2,1)} %bitcast.325), channel_id=1, source_target_pairs={{0,4},{4,0},{8,12},{12,8},{1,5},{5,1},{9,13},{13,9},{2,6},{6,2},{1... | collective-permute-start | bytes 2359304 | tf_op jit(solution)/shard_map/ppermute | solution.py:16
  605.5 108.9 %collective-permute-start.10 = (bf16[256,1,256]{2,0,1:T(8,128)(2,1)}, bf16[256,1,256]{2,0,1:T(8,128)(2,1)S(1)}, u32[]{:S(2)}, u32[]{:S(2)}) collective-permute-start(bf16[256,1,256]{2,0,1:T(8,128)(2,1)} %constant_dynamic-slice_fusion.15), channel_id=1, source_target_pairs={{0,8},{4,12},{8,0},{12,4},{1,9},{5,13},{9,1},{13,5},{2,10},{6,14},... | collective-permute-start | bytes 393224 | tf_op jit(solution)/shard_map/ppermute | solution.py:16
  610.1 15.1 %collective-permute-start.13 = (bf16[1,256,1024]{2,1,0:T(8,128)(2,1)}, bf16[1,256,1024]{2,1,0:T(8,128)(2,1)}, u32[]{:S(2)}, u32[]{:S(2)}) collective-permute-start(bf16[1,256,1024]{2,1,0:T(8,128)(2,1)} %constant_dynamic-slice_fusion.14), channel_id=1, source_target_pairs={{0,8},{4,12},{8,0},{12,4},{1,9},{5,13},{9,1},{13,5},{2,10},{6,14},... | collective-permute-start | bytes 1572872 | tf_op jit(solution)/shard_map/ppermute | solution.py:16
  617.6 110.7 %reduce-scatter.23.cloned.1.call-start = ((), (), s32[]{:S(2)}) async-start(), calls=%async_computation.26 | async-start | bytes 1310720 | tf_op jit(solution)/shard_map/reduce_scatter | solution.py:56
  618.7 17.6 %collective-permute-start.18 = (bf16[1024,1,256]{2,0,1:T(8,128)(2,1)}, bf16[1024,1,256]{2,0,1:T(8,128)(2,1)S(1)}, u32[]{:S(2)}, u32[]{:S(2)}) collective-permute-start(bf16[1024,1,256]{2,0,1:T(8,128)(2,1)} %constant_dynamic-slice_fusion.10), channel_id=1, source_target_pairs={{0,8},{4,12},{8,0},{12,4},{1,9},{5,13},{9,1},{13,5},{2,10},{6,14},... | collective-permute-start | bytes 1572872 | tf_op jit(solution)/shard_map/ppermute | solution.py:16
  627.0 21.0 %collective-permute-start.16 = (bf16[256,1024]{1,0:T(8,128)(2,1)S(1)}, bf16[256,1024]{1,0:T(8,128)(2,1)}, u32[]{:S(2)}, u32[]{:S(2)}) collective-permute-start(bf16[256,1024]{1,0:T(8,128)(2,1)S(1)} %select_bitcast_fusion.1), channel_id=1, source_target_pairs={{0,16},{16,0},{1,17},{17,1},{2,18},{18,2},{3,19},{19,3},{4,20},{20... | collective-permute-start | bytes 1572872 | tf_op jit(solution)/shard_map/ppermute | solution.py:16
  629.4 87.5 %collective-permute-start.5 = (bf16[1,256,768]{1,2,0:T(8,128)(2,1)}, bf16[1,256,768]{1,2,0:T(8,128)(2,1)}, u32[]{:S(2)}, u32[]{:S(2)}) collective-permute-start(bf16[1,256,768]{1,2,0:T(8,128)(2,1)} %constant_dynamic-slice_fusion.21), channel_id=1, source_target_pairs={{0,8},{4,12},{8,0},{12,4},{1,9},{5,13},{9,1},{13,5},{2,10},{6,14},... | collective-permute-start | bytes 1179656 | tf_op jit(solution)/shard_map/ppermute | solution.py:16
  638.6 63.0 %collective-permute-start.21 = (bf16[1024,256]{1,0:T(8,128)(2,1)}, bf16[1024,256]{1,0:T(8,128)(2,1)}, u32[]{:S(2)}, u32[]{:S(2)}) collective-permute-start(bf16[1024,256]{1,0:T(8,128)(2,1)} %select_bitcast_fusion), channel_id=1, source_target_pairs={{0,16},{16,0},{1,17},{17,1},{2,18},{18,2},{3,19},{19,3},{4,20},{20... | collective-permute-start | bytes 1572872 | tf_op jit(solution)/shard_map/ppermute | solution.py:16
  682.0 4.2 collective-permute-start.22
  684.5 22.1 %collective-permute-start.7 = (bf16[256,2,256]{2,0,1:T(8,128)(2,1)}, bf16[256,2,256]{2,0,1:T(8,128)(2,1)}, u32[]{:S(2)}, u32[]{:S(2)}) collective-permute-start(bf16[256,2,256]{2,0,1:T(8,128)(2,1)} %bitcast.290), channel_id=1, source_target_pairs={{0,4},{4,0},{8,12},{12,8},{1,5},{5,1},{9,13},{13,9},{2,6},{6,2},{1... | collective-permute-start | bytes 786440 | tf_op jit(solution)/shard_map/ppermute | solution.py:16
  686.3 3.7 collective-permute-start.23
  690.0 4.2 collective-permute-start.24
  694.3 6.5 collective-permute-start.25
  700.9 8.9 %collective-permute-start.2 = (bf16[2,256,768]{1,2,0:T(8,128)(2,1)}, bf16[2,256,768]{1,2,0:T(8,128)(2,1)}, u32[]{:S(2)}, u32[]{:S(2)}) collective-permute-start(bf16[2,256,768]{1,2,0:T(8,128)(2,1)} %bitcast.326), channel_id=1, source_target_pairs={{0,4},{4,0},{8,12},{12,8},{1,5},{5,1},{9,13},{13,9},{2,6},{6,2},{1... | collective-permute-start | bytes 2359304 | tf_op jit(solution)/shard_map/ppermute | solution.py:16
  701.6 4.9 collective-permute-start.26
  708.3 6.1 collective-permute-start.8
  711.9 11.2 %collective-permute-start.3 = (bf16[1,256,768]{1,2,0:T(8,128)(2,1)}, bf16[1,256,768]{1,2,0:T(8,128)(2,1)S(1)}, u32[]{:S(2)}, u32[]{:S(2)}) collective-permute-start(bf16[1,256,768]{1,2,0:T(8,128)(2,1)} %constant_dynamic-slice_fusion.24), channel_id=1, source_target_pairs={{0,8},{4,12},{8,0},{12,4},{1,9},{5,13},{9,1},{13,5},{2,10},{6,14},... | collective-permute-start | bytes 1179656 | tf_op jit(solution)/shard_map/ppermute | solution.py:16
  715.4 11.2 %collective-permute-start.11 = (bf16[256,256]{1,0:T(8,128)(2,1)S(1)}, bf16[256,256]{1,0:T(8,128)(2,1)S(1)}, u32[]{:S(2)}, u32[]{:S(2)}) collective-permute-start(bf16[256,256]{1,0:T(8,128)(2,1)S(1)} %select_bitcast_fusion.3), channel_id=1, source_target_pairs={{0,16},{16,0},{1,17},{17,1},{2,18},{18,2},{3,19},{19,3},{4,20},{20... | collective-permute-start | bytes 393224 | tf_op jit(solution)/shard_map/ppermute | solution.py:16
  725.2 12.3 %collective-permute-start.6 = (bf16[256,768]{0,1:T(8,128)(2,1)}, bf16[256,768]{0,1:T(8,128)(2,1)}, u32[]{:S(2)}, u32[]{:S(2)}) collective-permute-start(bf16[256,768]{0,1:T(8,128)(2,1)} %select_bitcast_fusion.2), channel_id=1, source_target_pairs={{0,16},{16,0},{1,17},{17,1},{2,18},{18,2},{3,19},{19,3},{4,20},{20... | collective-permute-start | bytes 1179656 | tf_op jit(solution)/shard_map/ppermute | solution.py:16
  730.1 11.2 %collective-permute-start.1 = (bf16[128,1024]{1,0:T(8,128)(2,1)}, bf16[128,1024]{1,0:T(8,128)(2,1)}, u32[]{:S(2)}, u32[]{:S(2)}) collective-permute-start(bf16[128,1024]{1,0:T(8,128)(2,1)} %get-tuple-element.58), channel_id=1, source_target_pairs={{0,16},{16,0},{1,17},{17,1},{2,18},{18,2},{3,19},{19,3},{4,20},{20... | collective-permute-start | bytes 786440 | tf_op jit(solution)/shard_map/ppermute | solution.py:16
  (75 other events, 786.0 us)
Sparse Core Ops, SparseCore 0:
  10.2 30.6 all-gather.14
  43.4 32.0 all-gather.16
  77.4 23.4 all-gather.18
  103.6 27.2 reduce-scatter.8
  132.7 35.0 all-gather.36
  169.8 27.9 all-gather.20
  199.7 36.7 all-gather.22
  240.4 27.2 reduce-scatter.10
  270.3 26.4 all-gather.24
  314.1 26.6 reduce-scatter.12
  345.5 26.4 all-gather.26
  383.7 26.6 reduce-scatter.14
  413.4 26.4 all-gather.28
  447.9 26.6 reduce-scatter.16
  478.3 26.4 all-gather.30
  521.2 26.6 reduce-scatter.18
  550.5 26.4 all-gather.32
  585.5 26.6 reduce-scatter.20
  617.7 27.3 all-gather.34
  690.1 25.9 reduce-scatter.22

commit v2 on v1

--- a/solution.py
+++ b/solution.py
@@ -48,14 +48,50 @@
     return jnp.dot(left_side, right_side, preferred_element_type=jnp.float32)
 
 
-def gather_tokens(rows):
-    return lax.all_gather(rows, "tensor", axis=0, tiled=True)
-
-
-def scatter_tokens(partial):
-    return lax.psum_scatter(
-        partial.astype(LOW), "tensor", scatter_dimension=0, tiled=True
-    ).astype(jnp.float32)
+class Columns:
+    def gather(self, rows):
+        return lax.all_gather(rows, "tensor", axis=0, tiled=True)
+
+    def scatter(self, partial):
+        return lax.psum_scatter(
+            partial.astype(LOW), "tensor", scatter_dimension=0, tiled=True
+        ).astype(jnp.float32)
+
+    def to_heads(self, rows, micro):
+        parts = lax.axis_size("tensor")
+        width = rows.shape[-1]
+        shaped = rows.reshape(parts, micro, -1, width // HEAD_DIM, HEAD_DIM)
+        shaped = shaped.transpose(1, 3, 0, 2, 4)
+        return shaped.reshape(micro, width // HEAD_DIM, -1, HEAD_DIM)
+
+    def from_heads(self, block):
+        micro, heads, count, _ = block.shape
+        parts = lax.axis_size("tensor")
+        shaped = block.reshape(micro, heads, parts, count // parts, HEAD_DIM)
+        return shaped.transpose(2, 0, 3, 1, 4).reshape(micro * count, heads * HEAD_DIM)
+
+
+class Quads:
+    def gather(self, rows):
+        near = jnp.concatenate([rows, swapped(rows, "tensor", 1)], axis=0)
+        return jnp.concatenate([near, swapped(near, "dp", 1)], axis=0)
+
+    def scatter(self, partial):
+        low = partial.astype(LOW)
+        count = low.shape[0] // 2
+        near = partial[:count] + swapped(low[count:], "dp", 1).astype(jnp.float32)
+        count = count // 2
+        came = swapped(near[count:].astype(LOW), "tensor", 1)
+        return near[:count] + came.astype(jnp.float32)
+
+    def to_heads(self, rows, micro):
+        width = rows.shape[-1]
+        shaped = rows.reshape(micro, -1, width // HEAD_DIM, HEAD_DIM)
+        return shaped.transpose(0, 2, 1, 3)
+
+    def from_heads(self, block):
+        micro, heads, count, _ = block.shape
+        return block.transpose(0, 2, 1, 3).reshape(micro * count, heads * HEAD_DIM)
 
 
 def norm_forward(values, gain_row, shift_row):
@@ -80,21 +116,6 @@
     return 0.5 * (1.0 + lax.erf(values * ROOT_HALF)) + values * INV_ROOT_TWOPI * jnp.exp(
         -0.5 * values * values
     )
-
-
-def to_heads(rows, micro):
-    parts = lax.axis_size("tensor")
-    width = rows.shape[-1]
-    shaped = rows.reshape(parts, micro, -1, width // HEAD_DIM, HEAD_DIM)
-    shaped = shaped.transpose(1, 3, 0, 2, 4)
-    return shaped.reshape(micro, width // HEAD_DIM, -1, HEAD_DIM)
-
-
-def from_heads(block):
-    micro, heads, count, _ = block.shape
-    parts = lax.axis_size("tensor")
-    shaped = block.reshape(micro, heads, parts, count // parts, HEAD_DIM)
-    return shaped.transpose(2, 0, 3, 1, 4).reshape(micro * count, heads * HEAD_DIM)
 
 
 def attend(queries, key_rows, value_rows, allowed):
@@ -129,28 +150,28 @@
     grad_values = jnp.einsum(
         "mhqk,mhqe->mhke", probs.astype(LOW), grad_context, preferred_element_type=jnp.float32
     )
-    return [from_heads(member.astype(LOW)) for member in (grad_query, grad_keys, grad_values)]
-
-
-def layer_forward(current, micro, allowed, weights, vectors):
+    return [member.astype(LOW) for member in (grad_query, grad_keys, grad_values)]
+
+
+def layer_forward(move, current, micro, allowed, weights, vectors):
     w_qkv, w_o, w_in, w_out = weights
     gains, biases, query_bias, value_bias, local_hidden_bias = vectors
-    gathered = gather_tokens(current)
+    gathered = move.gather(current)
     width = query_bias.shape[0]
     projected = dot(gathered, w_qkv)
-    queries = to_heads((projected[:, :width] + query_bias).astype(LOW), micro)
-    key_rows = to_heads(projected[:, width : 2 * width].astype(LOW), micro)
-    value_rows = to_heads((projected[:, 2 * width :] + value_bias).astype(LOW), micro)
+    queries = move.to_heads((projected[:, :width] + query_bias).astype(LOW), micro)
+    key_rows = move.to_heads(projected[:, width : 2 * width].astype(LOW), micro)
+    value_rows = move.to_heads((projected[:, 2 * width :] + value_bias).astype(LOW), micro)
     context, probs = attend(queries, key_rows, value_rows, allowed)
-    context = from_heads(context)
-    mixed_rows = scatter_tokens(dot(context, w_o))
+    context = move.from_heads(context)
+    mixed_rows = move.scatter(dot_cols(context, w_o))
     normed, scaled_one, inverse_one = norm_forward(
         current.astype(jnp.float32) + mixed_rows + biases[2], gains[0], biases[3]
     )
-    spread_rows = gather_tokens(normed.astype(LOW))
+    spread_rows = move.gather(normed.astype(LOW))
     hidden = dot(spread_rows, w_in) + local_hidden_bias
     active = jax.nn.gelu(hidden, approximate=False).astype(LOW)
-    branch = scatter_tokens(dot(active, w_out))
+    branch = move.scatter(dot_cols(active, w_out))
     final_rows, scaled_two, inverse_two = norm_forward(
         normed + branch + biases[4], gains[1], biases[5]
     )
@@ -161,7 +182,7 @@
     return (final_rows.astype(LOW), kept)
 
 
-def layer_backward(upstream, kept, weights, gains):
+def layer_backward(move, upstream, kept, weights, gains):
     (
         gathered, queries, key_rows, value_rows, probs, context, scaled_one, inverse_one,
         spread_rows, hidden, active, scaled_two, inverse_two,
@@ -169,20 +190,21 @@
     micro = queries.shape[0]
     w_qkv, w_o, w_in, w_out = weights
     grad_second, gain_two, shift_two = norm_backward(upstream, scaled_two, inverse_two, gains[1])
-    grad_feed = gather_tokens(grad_second.astype(LOW))
-    grad_active = dot_cols(grad_feed, w_out)
+    grad_feed = move.gather(grad_second.astype(LOW))
+    grad_active = dot(grad_feed, w_out)
     grad_hidden = (grad_active * gelu_slope(hidden)).astype(LOW)
-    part = scatter_tokens(dot_cols(grad_hidden, w_in))
-    grad_w_out = dot_rows(active, grad_feed).astype(LOW)
+    part = move.scatter(dot_cols(grad_hidden, w_in))
+    grad_w_out = dot_rows(grad_feed, active).astype(LOW)
     grad_w_in = dot_rows(spread_rows, grad_hidden).astype(LOW)
     grad_normed = grad_second + part
     grad_first, gain_one, shift_one = norm_backward(grad_normed, scaled_one, inverse_one, gains[0])
-    grad_mix = gather_tokens(grad_first.astype(LOW))
-    grad_context = to_heads(dot_cols(grad_mix, w_o).astype(LOW), micro)
+    grad_mix = move.gather(grad_first.astype(LOW))
+    grad_context = move.to_heads(dot(grad_mix, w_o).astype(LOW), micro)
     pieces = attend_back(queries, key_rows, value_rows, probs, grad_context)
+    pieces = [move.from_heads(member) for member in pieces]
     grad_project = jnp.concatenate(pieces, axis=1)
-    part = scatter_tokens(dot_cols(grad_project, w_qkv))
-    grad_w_o = dot_rows(context, grad_mix).astype(LOW)
+    part = move.scatter(dot_cols(grad_project, w_qkv))
+    grad_w_o = dot_rows(grad_mix, context).astype(LOW)
     grad_w_qkv = dot_rows(gathered, grad_project).astype(LOW)
     grad_current = grad_first + part
     width = pieces[0].shape[1]
@@ -201,10 +223,111 @@
     )
 
 
+def flipped(array, axis, when):
+    return jnp.where(when, jnp.flip(array, axis), array)
+
+
+def pick(array, index):
+    return lax.dynamic_index_in_dim(array, index, 0, keepdims=False)
+
+
+def summed_pair(one, two, kind):
+    return (one.astype(jnp.float32) + two.astype(jnp.float32)).astype(kind)
+
+
+def one_way(block, source):
+    return lax.ppermute(block, "pipe", [(source, 1 - source)])
+
+
+class General:
+    move = Columns()
+
+    def __init__(self, micro, row_count):
+        self.micro, self.row_count = micro, row_count
+        self.half = lax.axis_index("pipe")
+        self.column = lax.axis_index("tensor")
+
+    def mine(self, array):
+        return lax.dynamic_slice_in_dim(array, self.half * self.micro, self.micro, 0)
+
+    def labels(self, segments):
+        return self.mine(segments)
+
+    def rows_in(self, array):
+        return self.mine(array).reshape(self.micro * self.row_count, -1)
+
+    def rows_out(self, rows):
+        return rows.reshape(self.micro, self.row_count, -1)
+
+    def weights(self, shard):
+        full = lax.all_gather(shard, ("pipe", "dp"), axis=0, tiled=True)
+        return full.reshape(2, -1, shard.shape[1])
+
+    def reduced(self, layer, grad):
+        parts = lax.axis_size("dp")
+        total = halve_sum(grad.reshape(parts, -1, grad.shape[1]), "dp", 0, LOW)
+        return summed_pair(total, one_way(total, 1 - layer), LOW)
+
+    def finished(self, totals):
+        return jnp.where(self.half == 0, totals[0], totals[1]).astype(jnp.float32)
+
+
+class Paired(General):
+    move = Quads()
+
+    def __init__(self, micro, row_count):
+        super().__init__(micro, row_count)
+        place = lax.axis_index("dp")
+        self.core, self.side = place % 2, place // 2
+        self.near, self.group = self.column % 2, self.column // 2
+        self.home = self.group == self.core
+        self.column = self.near + 2 * self.core
+
+    def labels(self, segments):
+        own = pick(segments, self.half * self.micro + self.group)
+        both = jnp.stack([own, swapped(own, "dp", 1)]).reshape(2, 2, 2, -1)
+        both = flipped(flipped(both, 1, self.group == 1), 2, self.near == 1)
+        return both.transpose(0, 2, 1, 3).reshape(2, -1)
+
+    def rows_in(self, array):
+        kept = pick(array, self.half * self.micro + self.group)
+        given = pick(array, self.half * self.micro + 1 - self.group)
+        return jnp.concatenate([kept, swapped(given, "tensor", 2)], axis=0)
+
+    def rows_out(self, rows):
+        own, away = rows[: self.row_count], rows[self.row_count :]
+        return flipped(jnp.stack([own, swapped(away, "tensor", 2)]), 0, self.group == 1)
+
+    def weights(self, shard):
+        far = swapped(shard, "tensor", 2)
+        want = jnp.where(self.home, shard, far)
+        given = jnp.where(self.home, far, shard)
+        pair = jnp.stack([want, swapped(given, "dp", 1)])
+        other = swapped(pair, "pipe", 1)
+        layers = []
+        for layer in range(2):
+            part = jnp.where(self.half == layer, pair, other)
+            full = jnp.stack([part, swapped(part, "dp", 2)])
+            full = flipped(flipped(full, 1, self.core == 1), 0, self.side == 1)
+            layers.append(full.reshape(-1, shard.shape[1]))
+        return layers
+
+    def reduced(self, layer, grad):
+        split = grad.reshape(2, 2, -1, grad.shape[1])
+        came = swapped(pick(split, 1 - self.side), "dp", 2)
+        total = summed_pair(pick(split, self.side), came, LOW)
+        return summed_pair(total, one_way(total, 1 - layer), LOW)
+
+    def finished(self, totals):
+        mine = jnp.where(self.half == 0, totals[0], totals[1])
+        kept = pick(mine, self.core)
+        came = swapped(pick(mine, 1 - self.core), "dp", 1)
+        own = jnp.where(self.home, kept, came)
+        away = jnp.where(self.home, came, kept)
+        return summed_pair(own, swapped(away, "tensor", 2), jnp.float32)
+
+
 def body(inputs, segments, cotangent, w_qkv, w_o, w_in, w_out, ln_gains, model_biases, hidden_bias):
-    half = lax.axis_index("pipe")
-    first = half == 0
-    column = lax.axis_index("tensor")
     sections = lax.axis_size("pipe")
     parts = lax.axis_size("dp")
     columns = lax.axis_size("tensor")
@@ -215,65 +338,57 @@
     hidden_local = w_in.shape[-1]
     hidden_width = hidden_bias.shape[-1]
     block = w_qkv.shape[1]
-
-    shards = (
-        w_qkv[0].reshape(block, 3 * width), w_o[0].T, w_in[0], w_out[0].T
-    )
+    paired = parts == 4 and columns == 4 and micro == 2
+    plan = (Paired if paired else General)(micro, row_count)
+    first = plan.half == 0
+    column = plan.column
+
+    vector_own = jnp.concatenate([ln_gains[0].reshape(-1), model_biases[0].reshape(-1), hidden_bias[0]])
+    vector_other = swapped(vector_own, "pipe", 1)
+    labels = plan.labels(segments)
+    current = plan.rows_in(inputs)
     stacks = [
-        lax.all_gather(shard, ("pipe", "dp"), axis=0, tiled=True).reshape(
-            sections, parts * shard.shape[0], shard.shape[1]
-        )
-        for shard in shards
+        plan.weights(w_qkv[0].reshape(block, 3 * width)),
+        plan.weights(w_o[0].T),
+        plan.weights(w_in[0]),
+        plan.weights(w_out[0].T),
     ]
-    gains_all = lax.all_gather(ln_gains[0], "pipe")
-    biases_all = lax.all_gather(model_biases[0], "pipe")
-    hidden_all = lax.all_gather(hidden_bias[0], "pipe")
-
-    def own_slice(array, size, dim):
-        return lax.dynamic_slice_in_dim(array, column * size, size, dim)
-
-    def own_micro(array):
-        return lax.dynamic_slice_in_dim(array, half * micro, micro, 0)
-
-    labels = own_micro(segments)
+
+    def own_slice(array, size):
+        return lax.dynamic_slice_in_dim(array, column * size, size, 0)
+
     allowed = (labels[:, :, None] == labels[:, None, :])[:, None]
     weights, vectors = [], []
     for layer in range(sections):
-        weights.append(
-            (stacks[0][layer], stacks[1][layer].T, stacks[2][layer], stacks[3][layer].T)
-        )
-        biases = biases_all[layer]
+        weights.append(tuple(stack[layer] for stack in stacks))
+        flat = jnp.where(plan.half == layer, vector_own, vector_other)
+        gains = flat[: 2 * model_width].reshape(2, model_width)
+        biases = flat[2 * model_width : 8 * model_width].reshape(6, model_width)
         vectors.append(
             (
-                gains_all[layer], biases, own_slice(biases[0], width, 0),
-                own_slice(biases[1], width, 0), own_slice(hidden_all[layer], hidden_local, 0),
+                gains, biases, own_slice(biases[0], width), own_slice(biases[1], width),
+                own_slice(flat[8 * model_width :], hidden_local),
             )
         )
-    current = own_micro(inputs).reshape(micro * row_count, model_width)
     outs, kept_list = [], []
     for layer in range(sections):
-        current, kept = layer_forward(current, micro, allowed, weights[layer], vectors[layer])
-        outs.append(current)
+        current, kept = layer_forward(
+            plan.move, current, micro, allowed, weights[layer], vectors[layer]
+        )
+        outs.append(plan.rows_out(current))
         kept_list.append(kept)
-    upstream = own_micro(cotangent).reshape(micro * row_count, model_width)
+    upstream = plan.rows_in(cotangent)
     grads = [None] * sections
     totals = [None] * sections
     packs = [None] * sections
     zero = jnp.zeros((), jnp.int32)
+    blocks = parts * columns
     for layer in reversed(range(sections)):
         upstream, weight_grads, vector_grads = layer_backward(
-            upstream.astype(jnp.float32), kept_list[layer], weights[layer], vectors[layer][0]
-        )
-        grads[layer] = upstream
-        shaped = (
-            weight_grads[0].reshape(parts, block, 3 * width),
-            weight_grads[1].reshape(width, parts, model_width // parts),
-            weight_grads[2].reshape(parts, block, hidden_local),
-            weight_grads[3].reshape(hidden_local, parts, model_width // parts),
-        )
-        totals[layer] = [
-            halve_sum(member, "dp", dim, LOW) for member, dim in zip(shaped, (0, 1, 0, 1))
-        ]
+            plan.move, upstream.astype(jnp.float32), kept_list[layer], weights[layer], vectors[layer][0]
+        )
+        grads[layer] = plan.rows_out(upstream)
+        totals[layer] = [plan.reduced(layer, member) for member in weight_grads]
         row_grads, query_grad, value_grad, hidden_grads = vector_grads
         placed = lax.dynamic_update_slice(
             jnp.zeros((2, model_width), jnp.float32),
@@ -283,7 +398,6 @@
         hidden_full = lax.dynamic_update_slice(
             jnp.zeros((hidden_width,), jnp.float32), hidden_grads, (column * hidden_local,)
         )
-        blocks = parts * columns
         packs[layer] = jnp.concatenate(
             [
                 jnp.concatenate([row_grads[:2], placed, row_grads[2:]], axis=0)
@@ -294,25 +408,20 @@
             ],
             axis=1,
         )
+    summed = [plan.finished([totals[0][index], totals[1][index]]) for index in range(4)]
 
     def exchanged(pair):
         return jnp.where(first, pair[0], pair[1]), swapped(jnp.where(first, pair[1], pair[0]), "pipe", 1)
 
-    summed = []
-    for index in range(4):
-        own, came = exchanged([totals[0][index], totals[1][index]])
-        summed.append(own.astype(jnp.float32) + came.astype(jnp.float32))
     own, came = exchanged(packs)
     pack = (own + came).reshape(parts, columns, -1)
     pack = halve_sum(pack, "dp", 0, jnp.float32)
     pack = halve_sum(pack, "tensor", 0, jnp.float32)
-    rows_each = model_width // (parts * columns)
+    rows_each = model_width // blocks
     vector_part = pack[: 8 * rows_each].reshape(8, rows_each)
 
     def both_halves(pair):
         own, came = exchanged(pair)
-        shape = (micro, row_count, model_width)
-        own, came = own.reshape(shape), came.reshape(shape)
         return jnp.concatenate(
             [jnp.where(first, own, came), jnp.where(first, came, own)], axis=0
         )[None]
@@ -321,9 +430,9 @@
         both_halves(outs),
         both_halves(grads),
         summed[0].reshape(1, block, 3, width),
-        summed[1][None],
+        summed[1].T[None],
         summed[2][None],
-        summed[3][None],
+        summed[3].T[None],
         vector_part[:2][None],
         vector_part[2:][None],
         pack[8 * rows_each :][None],

time: 761 us -> 710 us (0.933)
  starting transfers between devices: 22.5 us -> 94.7 us
  waiting for transfers between devices: 437 us -> 380 us
  local copies, waits for them, and re-layouts: 106 us -> 75.2 us
  matrix products: 91.5 us -> 75.6 us
  blocking collectives: 14.3 us -> 0 us
  between operations: 16.3 us -> 3.63 us
  other arithmetic: 62.2 us -> 74.5 us
    ppermute x27 -> x83, waiting for transfers between devices: 21.4 us -> 369 us  [swapped(): return lax.ppermute(block, axis, [(i, i ^ bit) for i in range(size)])]
    all_gather x12 -> x0, waiting for transfers between devices: 275 us -> none  [the longest x8 168 us: gather_tokens(): return lax.all_gather(rows, 'tensor', axis=0, tiled=True)]
    reduce_scatter x8 -> x0, waiting for transfers between devices: 138 us -> none  [scatter_tokens(): lax.psum_scatter(partial.astype(LOW), 'tensor', scatter_dimension=0, tile...]
    ppermute x27 -> x83, starting transfers between devices: 20.4 us -> 78 us  [swapped(): return lax.ppermute(block, axis, [(i, i ^ bit) for i in range(size)])]
    select_n x0 -> x26, other arithmetic: none -> 26 us  [the longest x13 11.8 us: flipped(): return jnp.where(when, jnp.flip(array, axis), array)]
    reshape x40 -> x10, local copies, waits for them, and re-layouts: 28.8 us -> 4.25 us  [to_heads(): shaped = rows.reshape(micro, -1, width // HEAD_DIM, HEAD_DIM)]
    ppermute x0 -> x8, starting transfers between devices: none -> 16.7 us  [one_way(): return lax.ppermute(block, 'pipe', [(source, 1 - source)])]
    all_gather x3 -> x0, blocking collectives: 14.3 us -> none  [the longest x1 5.51 us: body(): biases_all = lax.all_gather(model_biases[0], 'pipe')]
  transfers between devices with their start and end apart: 47 -> 91, of which waited for: 24 -> 49; matrix products, arithmetic and copies ran while one was open for 26% -> 25% of each run, Pallas kernels for 0% -> 0%
where the time goes in v2:
time: 710 us; the launch traced here: 704 us
  waiting for transfers between devices  380 us (54%)
  starting transfers between devices  94.7 us (13%)
  matrix products  75.6 us (11%)
  local copies, waits for them, and re-layouts  75.2 us (11%)
  other arithmetic  74.5 us (10%)
    ppermute x83, waiting for transfers between devices, swapped(): return lax.ppermute(block, axis, [(i, i ^ bit) for i in range(size)])  369 us
    ppermute x83, starting transfers between devices, swapped(): return lax.ppermute(block, axis, [(i, i ^ bit) for i in range(size)])  78 us
    dot_general x8, matrix products, dot(): return jnp.dot(left_side, right_side, preferred_element_type=jnp.float32)  32.4 us
    unnamed x319, local copies, waits for them, and re-layouts  22 us
    dot_general x8, matrix products, dot_rows(): lax.dot_general(left_side, right_side, (((0,), (0,)), ((), ())), preferre...  17.6 us
    ppermute x8, starting transfers between devices, one_way(): return lax.ppermute(block, 'pipe', [(source, 1 - source)])  16.7 us
    convert_element_type x8, other arithmetic, summed_pair(): return (one.astype(jnp.float32) + two.astype(jnp.float32)).astype(kind)  15.6 us
  transfers between devices with their start and end apart: 91, of which 49 were waited for; matrix products, arithmetic and copies ran while one was open for 25% of the time, Pallas kernels for 0%

profile of v2, /device:TPU:0, one launch (start us, length us, event | category | flops | bytes accessed | tf_op | source)
XLA Modules:
  0.0 703.9 jit_solution(14135569527578701102)
XLA Ops:
  2.0 4.1 collective-permute-start.21
  20.2 46.5 %collective-permute-done = bf16[64,1024]{1,0:T(8,128)(2,1)S(1)} collective-permute-done((bf16[64,1024]{1,0:T(8,128)(2,1)S(1)}, bf16[64,1024]{1,0:T(8,128)(2,1)S(1)}, u32[]{:S(2)}, u32[]{:S(2)}) %collective-permute-start) | collective-permute-done | bytes 131104 | tf_op jit(solution)/shard_map/ppermute | solution.py:16
  72.9 12.6 %collective-permute-done.2 = bf16[128,1024]{1,0:T(8,128)(2,1)S(1)} collective-permute-done((bf16[128,1024]{1,0:T(8,128)(2,1)S(1)}, bf16[128,1024]{1,0:T(8,128)(2,1)S(1)}, u32[]{:S(2)}, u32[]{:S(2)}) %collective-permute-start.2) | collective-permute-done | bytes 262176 | tf_op jit(solution)/shard_map/ppermute | solution.py:16
  90.9 7.1 %collective-permute-done.12 = bf16[2,256,256]{2,1,0:T(8,128)(2,1)S(1)} collective-permute-done((bf16[2,256,256]{2,1,0:T(8,128)(2,1)S(1)}, bf16[2,256,256]{2,1,0:T(8,128)(2,1)S(1)}, u32[]{:S(2)}, u32[]{:S(2)}) %collective-permute-start.12) | collective-permute-done | bytes 262176 | tf_op jit(solution)/shard_map/ppermute | solution.py:16
  98.7 3.7 collective-permute-done.31
  102.5 5.1 collective-permute-done.6
  114.3 15.7 %collective-permute-done.23 = bf16[2,256,1024]{2,1,0:T(8,128)(2,1)S(1)} collective-permute-done((bf16[2,256,1024]{2,1,0:T(8,128)(2,1)S(1)}, bf16[2,256,1024]{2,1,0:T(8,128)(2,1)S(1)}, u32[]{:S(2)}, u32[]{:S(2)}) %collective-permute-start.23) | collective-permute-done | bytes 1048608 | tf_op jit(solution)/shard_map/ppermute | solution.py:16
  133.8 11.3 %collective-permute-done.30 = bf16[2,256,768]{1,2,0:T(8,128)(2,1)S(1)} collective-permute-done((bf16[2,256,768]{1,2,0:T(8,128)(2,1)S(1)}, bf16[2,256,768]{1,2,0:T(8,128)(2,1)S(1)}, u32[]{:S(2)}, u32[]{:S(2)}) %collective-permute-start.30) | collective-permute-done | bytes 786464 | tf_op jit(solution)/shard_map/ppermute | solution.py:16
  169.3 20.7 %collective-permute-done.37 = bf16[2,256,1024]{2,1,0:T(8,128)(2,1)} collective-permute-done((bf16[2,256,1024]{2,1,0:T(8,128)(2,1)}, bf16[2,256,1024]{2,1,0:T(8,128)(2,1)}, u32[]{:S(2)}, u32[]{:S(2)}) %collective-permute-start.37) | collective-permute-done | bytes 1048608 | tf_op jit(solution)/shard_map/ppermute | solution.py:16
  194.3 18.1 %collective-permute-done.20 = bf16[2,256,1024]{2,1,0:T(8,128)(2,1)S(1)} collective-permute-done((bf16[2,256,1024]{2,1,0:T(8,128)(2,1)S(1)}, bf16[2,256,1024]{2,1,0:T(8,128)(2,1)S(1)}, u32[]{:S(2)}, u32[]{:S(2)}) %collective-permute-start.20) | collective-permute-done | bytes 1048608 | tf_op jit(solution)/shard_map/ppermute | solution.py:16
  212.6 19.6 %collective-permute-done.36 = bf16[2,256,1024]{2,1,0:T(8,128)(2,1)S(1)} collective-permute-done((bf16[2,256,1024]{2,1,0:T(8,128)(2,1)S(1)}, bf16[2,256,1024]{2,1,0:T(8,128)(2,1)S(1)}, u32[]{:S(2)}, u32[]{:S(2)}) %collective-permute-start.36) | collective-permute-done | bytes 1048608 | tf_op jit(solution)/shard_map/ppermute | solution.py:16
  235.7 3.8 collective-permute-done.15
  241.5 8.1 %fusion.4 = (bf16[512,1024]{1,0:T(8,128)(2,1)S(1)}, f32[512,1024]{1,0:T(8,128)}) fusion(f32[1024]{0:T(1024)S(1)} %dynamic_slice.138, bf16[1024,1024]{1,0:T(8,128)(2,1)S(1)} %bitcast.335, bf16[256,1024]{1,0:T(8,128)(2,1)S(1)} %collective-permute-done.16, bf16[128,1024]{1,0:T(8,128)(2,1)S(1)} %collective-permute-done.15, bf16[128,1024]{1,0:T(8,128)(2,1)S(1)} %fusion.99), kind=kOutput, calls=%fused_computation.20 | convolution fusion | flops 1111490560 | bytes 6295552 | tf_op jit(solution)/shard_map/dot_general | solution.py:48
  253.3 8.3 %collective-permute-done.26 = bf16[128,1024]{1,0:T(8,128)(2,1)S(1)} collective-permute-done((bf16[128,1024]{1,0:T(8,128)(2,1)S(1)}, bf16[128,1024]{1,0:T(8,128)(2,1)S(1)}, u32[]{:S(2)}, u32[]{:S(2)}) %collective-permute-start.26) | collective-permute-done | bytes 262176 | tf_op jit(solution)/shard_map/ppermute | solution.py:16
  262.9 7.1 %collective-permute-done.28 = bf16[128,1024]{1,0:T(8,128)(2,1)S(1)} collective-permute-done((bf16[128,1024]{1,0:T(8,128)(2,1)S(1)}, bf16[128,1024]{1,0:T(8,128)(2,1)S(1)}, u32[]{:S(2)}, u32[]{:S(2)}) %collective-permute-start.28) | collective-permute-done | bytes 262176 | tf_op jit(solution)/shard_map/ppermute | solution.py:16
  287.1 8.0 %collective-permute-done.33 = bf16[128,1024]{1,0:T(8,128)(2,1)S(1)} collective-permute-done((bf16[128,1024]{1,0:T(8,128)(2,1)S(1)}, bf16[128,1024]{1,0:T(8,128)(2,1)S(1)}, u32[]{:S(2)}, u32[]{:S(2)}) %collective-permute-start.33) | collective-permute-done | bytes 262176 | tf_op jit(solution)/shard_map/ppermute | solution.py:16
  296.5 7.2 %collective-permute-done.34 = bf16[128,1024]{1,0:T(8,128)(2,1)S(1)} collective-permute-done((bf16[128,1024]{1,0:T(8,128)(2,1)S(1)}, bf16[128,1024]{1,0:T(8,128)(2,1)S(1)}, u32[]{:S(2)}, u32[]{:S(2)}) %collective-permute-start.34) | collective-permute-done | bytes 262176 | tf_op jit(solution)/shard_map/ppermute | solution.py:16
  306.0 7.9 %fusion.7 = (bf16[512,1024]{1,0:T(8,128)(2,1)S(1)}, f32[512,1024]{1,0:T(8,128)}) fusion(f32[1024]{0:T(1024)S(1)} %dynamic_slice.141, bf16[1024,1024]{1,0:T(8,128)(2,1)S(1)} %bitcast.339, bf16[256,1024]{1,0:T(8,128)(2,1)S(1)} %collective-permute-done.35, bf16[128,1024]{1,0:T(8,128)(2,1)S(1)} %collective-permute-done.34, bf16[128,1024]{1,0:T(8,128)(2,1)S(1)} %fusion.100), kind=kOutput, calls=%fused_computation.23 | convolution fusion | flops 1111490560 | bytes 6295552 | tf_op jit(solution)/shard_map/dot_general | solution.py:48
  318.3 3.6 collective-permute-start.42
  321.9 7.2 %collective-permute-done.39 = bf16[128,1024]{1,0:T(8,128)(2,1)S(1)} collective-permute-done((bf16[128,1024]{1,0:T(8,128)(2,1)S(1)}, bf16[128,1024]{1,0:T(8,128)(2,1)S(1)}, u32[]{:S(2)}, u32[]{:S(2)}) %collective-permute-start.39) | collective-permute-done | bytes 262176 | tf_op jit(solution)/shard_map/ppermute | solution.py:16
  336.2 6.1 collective-permute-done.43
  350.1 3.6 collective-permute-done.40
  357.0 4.5 convert_reduce_fusion
  373.0 4.0 collective-permute-done.46
  379.3 5.1 collective-permute-done.47
  384.5 9.6 %collective-permute-done.82 = bf16[2,256,1024]{2,1,0:T(8,128)(2,1)} collective-permute-done((bf16[2,256,1024]{2,1,0:T(8,128)(2,1)}, bf16[2,256,1024]{2,1,0:T(8,128)(2,1)}, u32[]{:S(2)}, u32[]{:S(2)}) %collective-permute-start.82) | collective-permute-done | bytes 1048608 | tf_op jit(solution)/shard_map/ppermute | solution.py:16
  397.1 3.7 collective-permute-start.83
  400.8 14.3 %collective-permute-done.76 = bf16[2,256,1024]{2,1,0:T(8,128)(2,1)} collective-permute-done((bf16[2,256,1024]{2,1,0:T(8,128)(2,1)}, bf16[2,256,1024]{2,1,0:T(8,128)(2,1)}, u32[]{:S(2)}, u32[]{:S(2)}) %collective-permute-start.76) | collective-permute-done | bytes 1048608 | tf_op jit(solution)/shard_map/ppermute | solution.py:16
  416.7 3.8 collective-permute-start.77
  444.8 7.1 %collective-permute-done.50 = bf16[128,1024]{1,0:T(8,128)(2,1)S(1)} collective-permute-done((bf16[128,1024]{1,0:T(8,128)(2,1)S(1)}, bf16[128,1024]{1,0:T(8,128)(2,1)S(1)}, u32[]{:S(2)}, u32[]{:S(2)}) %collective-permute-start.50) | collective-permute-done | bytes 262176 | tf_op jit(solution)/shard_map/ppermute | solution.py:16
  455.8 5.1 collective-permute-done.51
  470.4 4.5 convert_reduce_fusion.1
  491.0 4.3 collective-permute-done.54
  501.0 4.2 collective-permute-done.55
  505.3 4.7 collective-permute-done.80
  513.4 18.6 %collective-permute-done.74 = bf16[2,256,1024]{2,1,0:T(8,128)(2,1)} collective-permute-done((bf16[2,256,1024]{2,1,0:T(8,128)(2,1)}, bf16[2,256,1024]{2,1,0:T(8,128)(2,1)}, u32[]{:S(2)}, u32[]{:S(2)}) %collective-permute-start.74) | collective-permute-done | bytes 1048608 | tf_op jit(solution)/shard_map/ppermute | solution.py:16
  546.9 3.7 collective-permute-start.86
  550.6 4.0 fusion.210
  554.6 7.9 %collective-permute-done.86 = f32[16,768]{1,0:T(8,128)S(1)} collective-permute-done((f32[16,768]{1,0:T(8,128)S(1)}, f32[16,768]{1,0:T(8,128)S(1)}, u32[]{:S(2)}, u32[]{:S(2)}) %collective-permute-start.86) | collective-permute-done | bytes 49184 | tf_op jit(solution)/shard_map/ppermute | solution.py:16
  562.7 3.7 convolution_convert_fusion.5
  587.4 3.3 collective-permute-done.68
  606.6 4.3 collective-permute-done.69
  617.3 7.1 %collective-permute-done.58 = bf16[128,1024]{1,0:T(8,128)(2,1)S(1)} collective-permute-done((bf16[128,1024]{1,0:T(8,128)(2,1)S(1)}, bf16[128,1024]{1,0:T(8,128)(2,1)S(1)}, u32[]{:S(2)}, u32[]{:S(2)}) %collective-permute-start.58) | collective-permute-done | bytes 262176 | tf_op jit(solution)/shard_map/ppermute | solution.py:16
  627.5 6.8 collective-permute-done.59
  639.7 7.3 %collective-permute-done.63 = bf16[2,256,768]{1,2,0:T(8,128)(2,1)} collective-permute-done((bf16[2,256,768]{1,2,0:T(8,128)(2,1)}, bf16[2,256,768]{1,2,0:T(8,128)(2,1)}, u32[]{:S(2)}, u32[]{:S(2)}) %collective-permute-start.63) | collective-permute-done | bytes 786464 | tf_op jit(solution)/shard_map/ppermute | solution.py:239
  656.8 26.1 %collective-permute-done.85 = bf16[256,1024]{1,0:T(8,128)(2,1)S(1)} collective-permute-done((bf16[256,1024]{1,0:T(8,128)(2,1)S(1)}, bf16[256,1024]{1,0:T(8,128)(2,1)S(1)}, u32[]{:S(2)}, u32[]{:S(2)}) %collective-permute-start.85) | collective-permute-done | bytes 524320 | tf_op jit(solution)/shard_map/ppermute | solution.py:16
  686.7 7.5 %collective-permute-done.79 = bf16[256,1024]{1,0:T(8,128)(2,1)} collective-permute-done((bf16[256,1024]{1,0:T(8,128)(2,1)}, bf16[256,1024]{1,0:T(8,128)(2,1)}, u32[]{:S(2)}, u32[]{:S(2)}) %collective-permute-start.79) | collective-permute-done | bytes 524320 | tf_op jit(solution)/shard_map/ppermute | solution.py:16
  696.5 6.0 collective-permute-done.67
  (754 shorter events, 283.8 us)
Async XLA Ops:
  2.0 84.4 %collective-permute-start.21 = (bf16[256,1024]{1,0:T(8,128)(2,1)S(1)}, bf16[256,1024]{1,0:T(8,128)(2,1)S(1)}, u32[]{:S(2)}, u32[]{:S(2)}) collective-permute-start(bf16[256,1024]{1,0:T(8,128)(2,1)S(1)} %bitcast.326), channel_id=1, source_target_pairs={{0,2},{1,3},{2,0},{3,1},{4,6},{5,7},{6,4},{7,5},{8,10},{9,11},{10,... | collective-permute-start | bytes 1572872 | tf_op jit(solution)/shard_map/ppermute | solution.py:16
  7.3 62.4 %collective-permute-start.4 = (bf16[256,768]{0,1:T(8,128)(2,1)S(1)}, bf16[256,768]{0,1:T(8,128)(2,1)S(1)}, u32[]{:S(2)}, u32[]{:S(2)}) collective-permute-start(bf16[256,768]{0,1:T(8,128)(2,1)S(1)} %bitcast.357), channel_id=1, source_target_pairs={{0,2},{1,3},{2,0},{3,1},{4,6},{5,7},{6,4},{7,5},{8,10},{9,11},{10,... | collective-permute-start | bytes 1179656 | tf_op jit(solution)/shard_map/ppermute | solution.py:16
  8.4 58.2 %collective-permute-start = (bf16[64,1024]{1,0:T(8,128)(2,1)S(1)}, bf16[64,1024]{1,0:T(8,128)(2,1)S(1)}, u32[]{:S(2)}, u32[]{:S(2)}) collective-permute-start(bf16[64,1024]{1,0:T(8,128)(2,1)S(1)} %get-tuple-element.94), channel_id=1, source_target_pairs={{0,2},{1,3},{2,0},{3,1},{4,6},{5,7},{6,4},{7,5},{8,10},{9,11},{10,... | collective-permute-start | bytes 393224 | tf_op jit(solution)/shard_map/ppermute | solution.py:16
  16.0 53.5 %collective-permute-start.9 = (bf16[256,256]{1,0:T(8,128)(2,1)S(1)}, bf16[256,256]{1,0:T(8,128)(2,1)S(1)}, u32[]{:S(2)}, u32[]{:S(2)}) collective-permute-start(bf16[256,256]{1,0:T(8,128)(2,1)S(1)} %bitcast.391), channel_id=1, source_target_pairs={{0,2},{1,3},{2,0},{3,1},{4,6},{5,7},{6,4},{7,5},{8,10},{9,11},{10,... | collective-permute-start | bytes 393224 | tf_op jit(solution)/shard_map/ppermute | solution.py:16
  17.4 72.9 %collective-permute-start.17 = (bf16[256,1024]{1,0:T(8,128)(2,1)S(1)}, bf16[256,1024]{1,0:T(8,128)(2,1)S(1)}, u32[]{:S(2)}, u32[]{:S(2)}) collective-permute-start(bf16[256,1024]{1,0:T(8,128)(2,1)S(1)} %bitcast.390), channel_id=1, source_target_pairs={{0,2},{1,3},{2,0},{3,1},{4,6},{5,7},{6,4},{7,5},{8,10},{9,11},{10,... | collective-permute-start | bytes 1572872 | tf_op jit(solution)/shard_map/ppermute | solution.py:16
  66.7 18.8 %collective-permute-start.2 = (bf16[128,1024]{1,0:T(8,128)(2,1)S(1)}, bf16[128,1024]{1,0:T(8,128)(2,1)S(1)}, u32[]{:S(2)}, u32[]{:S(2)}) collective-permute-start(bf16[128,1024]{1,0:T(8,128)(2,1)S(1)} %pad_maximum_fusion.41), channel_id=1, source_target_pairs={{0,1},{1,0},{2,3},{3,2},{4,5},{5,4},{6,7},{7,6},{8,9},{9,8},{10,11... | collective-permute-start | bytes 786440 | tf_op jit(solution)/shard_map/ppermute | solution.py:16
  69.8 17.2 %collective-permute-start.5 = (bf16[256,768]{0,1:T(8,128)(2,1)S(1)}, bf16[256,768]{0,1:T(8,128)(2,1)S(1)}, u32[]{:S(2)}, u32[]{:S(2)}) collective-permute-start(bf16[256,768]{0,1:T(8,128)(2,1)S(1)} %get-tuple-element.87), channel_id=1, source_target_pairs={{0,4},{4,0},{8,12},{12,8},{1,5},{5,1},{9,13},{13,9},{2,6},{6,2},{1... | collective-permute-start | bytes 1179656 | tf_op jit(solution)/shard_map/ppermute | solution.py:16
  71.0 17.7 %collective-permute-start.11 = (bf16[2,256,256]{2,1,0:T(8,128)(2,1)S(1)}, bf16[2,256,256]{2,1,0:T(8,128)(2,1)S(1)}, u32[]{:S(2)}, u32[]{:S(2)}) collective-permute-start(bf16[2,256,256]{2,1,0:T(8,128)(2,1)S(1)} %pad_maximum_fusion.42), channel_id=1, source_target_pairs={{0,16},{16,0},{1,17},{17,1},{2,18},{18,2},{3,19},{19,3},{4,20},{20... | collective-permute-start | bytes 786440 | tf_op jit(solution)/shard_map/ppermute | solution.py:16
  86.4 62.8 %collective-permute-start.3 = (bf16[256,1024]{1,0:T(8,128)(2,1)}, bf16[256,1024]{1,0:T(8,128)(2,1)}, u32[]{:S(2)}, u32[]{:S(2)}) collective-permute-start(bf16[256,1024]{1,0:T(8,128)(2,1)} %pad_maximum_fusion.17), channel_id=1, source_target_pairs={{0,4},{4,0},{8,12},{12,8},{1,5},{5,1},{9,13},{13,9},{2,6},{6,2},{1... | collective-permute-start | bytes 1572872 | tf_op jit(solution)/shard_map/ppermute | solution.py:16
  86.5 11.6 %collective-permute-start.22 = (bf16[256,1024]{1,0:T(8,128)(2,1)S(1)}, bf16[256,1024]{1,0:T(8,128)(2,1)S(1)}, u32[]{:S(2)}, u32[]{:S(2)}) collective-permute-start(bf16[256,1024]{1,0:T(8,128)(2,1)S(1)} %get-tuple-element.79), channel_id=1, source_target_pairs={{0,4},{4,0},{8,12},{12,8},{1,5},{5,1},{9,13},{13,9},{2,6},{6,2},{1... | collective-permute-start | bytes 1572872 | tf_op jit(solution)/shard_map/ppermute | solution.py:16
  87.1 20.5 %collective-permute-start.6 = (bf16[2,256,768]{1,2,0:T(8,128)(2,1)S(1)}, bf16[2,256,768]{1,2,0:T(8,128)(2,1)S(1)}, u32[]{:S(2)}, u32[]{:S(2)}) collective-permute-start(bf16[2,256,768]{1,2,0:T(8,128)(2,1)S(1)} %pad_maximum_fusion.16), channel_id=1, source_target_pairs={{0,16},{16,0},{1,17},{17,1},{2,18},{18,2},{3,19},{19,3},{4,20},{20... | collective-permute-start | bytes 2359304 | tf_op jit(solution)/shard_map/ppermute | solution.py:16
  90.3 12.1 %collective-permute-start.31 = (bf16[2,256,256]{2,1,0:T(8,128)(2,1)S(1)}, bf16[2,256,256]{2,1,0:T(8,128)(2,1)S(1)}, u32[]{:S(2)}, u32[]{:S(2)}) collective-permute-start(bf16[2,256,256]{2,1,0:T(8,128)(2,1)S(1)} %get-tuple-element.91), channel_id=1, source_target_pairs={{0,8},{4,12},{8,0},{12,4},{1,9},{5,13},{9,1},{13,5},{2,10},{6,14},... | collective-permute-start | bytes 786440 | tf_op jit(solution)/shard_map/ppermute | solution.py:16
  98.0 13.0 %collective-permute-start.18 = (bf16[256,1024]{1,0:T(8,128)(2,1)S(1)}, bf16[256,1024]{1,0:T(8,128)(2,1)S(1)}, u32[]{:S(2)}, u32[]{:S(2)}) collective-permute-start(bf16[256,1024]{1,0:T(8,128)(2,1)S(1)} %get-tuple-element.81), channel_id=1, source_target_pairs={{0,4},{4,0},{8,12},{12,8},{1,5},{5,1},{9,13},{13,9},{2,6},{6,2},{1... | collective-permute-start | bytes 1572872 | tf_op jit(solution)/shard_map/ppermute | solution.py:16
  98.2 31.9 %collective-permute-start.23 = (bf16[2,256,1024]{2,1,0:T(8,128)(2,1)S(1)}, bf16[2,256,1024]{2,1,0:T(8,128)(2,1)S(1)}, u32[]{:S(2)}, u32[]{:S(2)}) collective-permute-start(bf16[2,256,1024]{2,1,0:T(8,128)(2,1)S(1)} %pad_maximum_fusion.9), channel_id=1, source_target_pairs={{0,16},{16,0},{1,17},{17,1},{2,18},{18,2},{3,19},{19,3},{4,20},{20... | collective-permute-start | bytes 3145736 | tf_op jit(solution)/shard_map/ppermute | solution.py:16
  107.7 25.5 %collective-permute-start.7 = (bf16[2,256,768]{1,2,0:T(8,128)(2,1)S(1)}, bf16[2,256,768]{1,2,0:T(8,128)(2,1)S(1)}, u32[]{:S(2)}, u32[]{:S(2)}) collective-permute-start(bf16[2,256,768]{1,2,0:T(8,128)(2,1)S(1)} %get-tuple-element.75), channel_id=1, source_target_pairs={{0,8},{4,12},{8,0},{12,4},{1,9},{5,13},{9,1},{13,5},{2,10},{6,14},... | collective-permute-start | bytes 2359304 | tf_op jit(solution)/shard_map/ppermute | solution.py:16
  109.5 35.5 %collective-permute-start.30 = (bf16[2,256,768]{1,2,0:T(8,128)(2,1)S(1)}, bf16[2,256,768]{1,2,0:T(8,128)(2,1)S(1)}, u32[]{:S(2)}, u32[]{:S(2)}) collective-permute-start(bf16[2,256,768]{1,2,0:T(8,128)(2,1)S(1)} %get-tuple-element.74), channel_id=1, source_target_pairs={{0,8},{4,12},{8,0},{12,4},{1,9},{5,13},{9,1},{13,5},{2,10},{6,14},... | collective-permute-start | bytes 2359304 | tf_op jit(solution)/shard_map/ppermute | solution.py:16
  112.8 49.3 %collective-permute-start.19 = (bf16[2,256,1024]{2,1,0:T(8,128)(2,1)}, bf16[2,256,1024]{2,1,0:T(8,128)(2,1)}, u32[]{:S(2)}, u32[]{:S(2)}) collective-permute-start(bf16[2,256,1024]{2,1,0:T(8,128)(2,1)} %pad_maximum_fusion.8), channel_id=1, source_target_pairs={{0,16},{16,0},{1,17},{17,1},{2,18},{18,2},{3,19},{19,3},{4,20},{20... | collective-permute-start | bytes 3145736 | tf_op jit(solution)/shard_map/ppermute | solution.py:16
  131.6 36.0 %collective-permute-start.24 = (bf16[2,256,1024]{2,1,0:T(8,128)(2,1)}, bf16[2,256,1024]{2,1,0:T(8,128)(2,1)}, u32[]{:S(2)}, u32[]{:S(2)}) collective-permute-start(bf16[2,256,1024]{2,1,0:T(8,128)(2,1)} %get-tuple-element.65), channel_id=1, source_target_pairs={{0,8},{4,12},{8,0},{12,4},{1,9},{5,13},{9,1},{13,5},{2,10},{6,14},... | collective-permute-start | bytes 3145736 | tf_op jit(solution)/shard_map/ppermute | solution.py:16
  133.2 56.9 %collective-permute-start.37 = (bf16[2,256,1024]{2,1,0:T(8,128)(2,1)}, bf16[2,256,1024]{2,1,0:T(8,128)(2,1)}, u32[]{:S(2)}, u32[]{:S(2)}) collective-permute-start(bf16[2,256,1024]{2,1,0:T(8,128)(2,1)} %get-tuple-element.64), channel_id=1, source_target_pairs={{0,8},{4,12},{8,0},{12,4},{1,9},{5,13},{9,1},{13,5},{2,10},{6,14},... | collective-permute-start | bytes 3145736 | tf_op jit(solution)/shard_map/ppermute | solution.py:16
  163.6 48.8 %collective-permute-start.20 = (bf16[2,256,1024]{2,1,0:T(8,128)(2,1)S(1)}, bf16[2,256,1024]{2,1,0:T(8,128)(2,1)S(1)}, u32[]{:S(2)}, u32[]{:S(2)}) collective-permute-start(bf16[2,256,1024]{2,1,0:T(8,128)(2,1)S(1)} %get-tuple-element.67), channel_id=1, source_target_pairs={{0,8},{4,12},{8,0},{12,4},{1,9},{5,13},{9,1},{13,5},{2,10},{6,14},... | collective-permute-start | bytes 3145736 | tf_op jit(solution)/shard_map/ppermute | solution.py:16
  165.3 66.9 %collective-permute-start.36 = (bf16[2,256,1024]{2,1,0:T(8,128)(2,1)S(1)}, bf16[2,256,1024]{2,1,0:T(8,128)(2,1)S(1)}, u32[]{:S(2)}, u32[]{:S(2)}) collective-permute-start(bf16[2,256,1024]{2,1,0:T(8,128)(2,1)S(1)} %get-tuple-element.66), channel_id=1, source_target_pairs={{0,8},{4,12},{8,0},{12,4},{1,9},{5,13},{9,1},{13,5},{2,10},{6,14},... | collective-permute-start | bytes 3145736 | tf_op jit(solution)/shard_map/ppermute | solution.py:16
  166.9 65.4 %collective-permute-start.14 = (bf16[128,1024]{1,0:T(8,128)(2,1)S(1)}, bf16[128,1024]{1,0:T(8,128)(2,1)S(1)}, u32[]{:S(2)}, u32[]{:S(2)}) collective-permute-start(bf16[128,1024]{1,0:T(8,128)(2,1)S(1)} %slice.512), channel_id=1, source_target_pairs={{0,1},{1,0},{2,3},{3,2},{4,5},{5,4},{6,7},{7,6},{8,9},{9,8},{10,11... | collective-permute-start | bytes 786440 | tf_op jit(solution)/shard_map/ppermute | solution.py:16
  317.7 11.5 %collective-permute-start.39 = (bf16[128,1024]{1,0:T(8,128)(2,1)S(1)}, bf16[128,1024]{1,0:T(8,128)(2,1)S(1)}, u32[]{:S(2)}, u32[]{:S(2)}) collective-permute-start(bf16[128,1024]{1,0:T(8,128)(2,1)S(1)} %slice.508), channel_id=1, source_target_pairs={{0,1},{1,0},{2,3},{3,2},{4,5},{5,4},{6,7},{7,6},{8,9},{9,8},{10,11... | collective-permute-start | bytes 786440 | tf_op jit(solution)/shard_map/ppermute | solution.py:16
  318.3 11.4 %collective-permute-start.42 = (bf16[64,1024]{1,0:T(8,128)(2,1)S(1)}, bf16[64,1024]{1,0:T(8,128)(2,1)S(1)}, u32[]{:S(2)}, u32[]{:S(2)}) collective-permute-start(bf16[64,1024]{1,0:T(8,128)(2,1)S(1)} %get-tuple-element.90), channel_id=1, source_target_pairs={{0,2},{1,3},{2,0},{3,1},{4,6},{5,7},{6,4},{7,5},{8,10},{9,11},{10,... | collective-permute-start | bytes 393224 | tf_op jit(solution)/shard_map/ppermute | solution.py:16
  343.2 13.8 %collective-permute-start.44 = (bf16[256,1024]{1,0:T(8,128)(2,1)}, bf16[256,1024]{1,0:T(8,128)(2,1)}, u32[]{:S(2)}, u32[]{:S(2)}) collective-permute-start(bf16[256,1024]{1,0:T(8,128)(2,1)} %pad_maximum_fusion.23), channel_id=1, source_target_pairs={{0,4},{4,0},{8,12},{12,8},{1,5},{5,1},{9,13},{13,9},{2,6},{6,2},{1... | collective-permute-start | bytes 1572872 | tf_op jit(solution)/shard_map/ppermute | solution.py:16
  367.7 26.3 %collective-permute-start.82 = (bf16[2,256,1024]{2,1,0:T(8,128)(2,1)}, bf16[2,256,1024]{2,1,0:T(8,128)(2,1)}, u32[]{:S(2)}, u32[]{:S(2)}) collective-permute-start(bf16[2,256,1024]{2,1,0:T(8,128)(2,1)} %dynamic-slice_bitcast_fusion), channel_id=1, source_target_pairs={{0,8},{4,12},{8,0},{12,4},{1,9},{5,13},{9,1},{13,5},{2,10},{6,14},... | collective-permute-start | bytes 3145736 | tf_op jit(solution)/shard_map/ppermute | solution.py:16
  372.1 43.0 %collective-permute-start.76 = (bf16[2,256,1024]{2,1,0:T(8,128)(2,1)}, bf16[2,256,1024]{2,1,0:T(8,128)(2,1)}, u32[]{:S(2)}, u32[]{:S(2)}) collective-permute-start(bf16[2,256,1024]{2,1,0:T(8,128)(2,1)} %dynamic-slice_bitcast_fusion.2), channel_id=1, source_target_pairs={{0,8},{4,12},{8,0},{12,4},{1,9},{5,13},{9,1},{13,5},{2,10},{6,14},... | collective-permute-start | bytes 3145736 | tf_op jit(solution)/shard_map/ppermute | solution.py:16
  384.4 36.1 %collective-permute-start.48 = (bf16[256,1024]{1,0:T(8,128)(2,1)S(1)}, bf16[256,1024]{1,0:T(8,128)(2,1)S(1)}, u32[]{:S(2)}, u32[]{:S(2)}) collective-permute-start(bf16[256,1024]{1,0:T(8,128)(2,1)S(1)} %pad_maximum_fusion.24), channel_id=1, source_target_pairs={{0,4},{4,0},{8,12},{12,8},{1,5},{5,1},{9,13},{13,9},{2,6},{6,2},{1... | collective-permute-start | bytes 1572872 | tf_op jit(solution)/shard_map/ppermute | solution.py:16
  397.1 196.3 %collective-permute-start.83 = (bf16[2,256,1024]{2,1,0:T(8,128)(2,1)}, bf16[2,256,1024]{2,1,0:T(8,128)(2,1)}, u32[]{:S(2)}, u32[]{:S(2)}) collective-permute-start(bf16[2,256,1024]{2,1,0:T(8,128)(2,1)} %fusion.18), channel_id=1, source_target_pairs={{0,16},{1,17},{2,18},{3,19},{4,20},{5,21},{6,22},{7,23},{8,24},{9,... | collective-permute-start | bytes 3145736 | tf_op jit(solution)/shard_map/ppermute | solution.py:239
  416.7 183.5 %collective-permute-start.77 = (bf16[2,256,1024]{2,1,0:T(8,128)(2,1)S(1)}, bf16[2,256,1024]{2,1,0:T(8,128)(2,1)}, u32[]{:S(2)}, u32[]{:S(2)}) collective-permute-start(bf16[2,256,1024]{2,1,0:T(8,128)(2,1)S(1)} %fusion.20), channel_id=1, source_target_pairs={{0,16},{1,17},{2,18},{3,19},{4,20},{5,21},{6,22},{7,23},{8,24},{9,... | collective-permute-start | bytes 3145736 | tf_op jit(solution)/shard_map/ppermute | solution.py:239
  440.2 27.7 %collective-permute-start.64 = (bf16[2,256,768]{1,2,0:T(8,128)(2,1)}, bf16[2,256,768]{1,2,0:T(8,128)(2,1)}, u32[]{:S(2)}, u32[]{:S(2)}) collective-permute-start(bf16[2,256,768]{1,2,0:T(8,128)(2,1)} %bitcast.387), channel_id=1, source_target_pairs={{0,8},{4,12},{8,0},{12,4},{1,9},{5,13},{9,1},{13,5},{2,10},{6,14},... | collective-permute-start | bytes 2359304 | tf_op jit(solution)/shard_map/ppermute | solution.py:16
  479.3 18.2 %collective-permute-start.60 = (bf16[64,1024]{1,0:T(8,128)(2,1)}, bf16[64,1024]{1,0:T(8,128)(2,1)S(1)}, u32[]{:S(2)}, u32[]{:S(2)}) collective-permute-start(bf16[64,1024]{1,0:T(8,128)(2,1)} %get-tuple-element.96), channel_id=1, source_target_pairs={{0,2},{1,3},{2,0},{3,1},{4,6},{5,7},{6,4},{7,5},{8,10},{9,11},{10,... | collective-permute-start | bytes 393224 | tf_op jit(solution)/shard_map/ppermute | solution.py:16
  483.6 26.4 %collective-permute-start.80 = (bf16[2,256,1024]{2,1,0:T(8,128)(2,1)}, bf16[2,256,1024]{2,1,0:T(8,128)(2,1)}, u32[]{:S(2)}, u32[]{:S(2)}) collective-permute-start(bf16[2,256,1024]{2,1,0:T(8,128)(2,1)} %dynamic-slice_bitcast_fusion.1), channel_id=1, source_target_pairs={{0,8},{4,12},{8,0},{12,4},{1,9},{5,13},{9,1},{13,5},{2,10},{6,14},... | collective-permute-start | bytes 3145736 | tf_op jit(solution)/shard_map/ppermute | solution.py:16
  495.3 36.7 %collective-permute-start.74 = (bf16[2,256,1024]{2,1,0:T(8,128)(2,1)}, bf16[2,256,1024]{2,1,0:T(8,128)(2,1)}, u32[]{:S(2)}, u32[]{:S(2)}) collective-permute-start(bf16[2,256,1024]{2,1,0:T(8,128)(2,1)} %dynamic-slice_bitcast_fusion.3), channel_id=1, source_target_pairs={{0,8},{4,12},{8,0},{12,4},{1,9},{5,13},{9,1},{13,5},{2,10},{6,14},... | collective-permute-start | bytes 3145736 | tf_op jit(solution)/shard_map/ppermute | solution.py:16
  505.2 30.7 %collective-permute-start.56 = (bf16[256,1024]{1,0:T(8,128)(2,1)S(1)}, bf16[256,1024]{1,0:T(8,128)(2,1)S(1)}, u32[]{:S(2)}, u32[]{:S(2)}) collective-permute-start(bf16[256,1024]{1,0:T(8,128)(2,1)S(1)} %pad_maximum_fusion.26), channel_id=1, source_target_pairs={{0,4},{4,0},{8,12},{12,8},{1,5},{5,1},{9,13},{13,9},{2,6},{6,2},{1... | collective-permute-start | bytes 1572872 | tf_op jit(solution)/shard_map/ppermute | solution.py:16
  512.0 83.7 %collective-permute-start.81 = (bf16[2,256,1024]{2,1,0:T(8,128)(2,1)S(1)}, bf16[2,256,1024]{2,1,0:T(8,128)(2,1)}, u32[]{:S(2)}, u32[]{:S(2)}) collective-permute-start(bf16[2,256,1024]{2,1,0:T(8,128)(2,1)S(1)} %fusion.19), channel_id=1, source_target_pairs={{16,0},{17,1},{18,2},{19,3},{20,4},{21,5},{22,6},{23,7},{24,8},{25... | collective-permute-start | bytes 3145736 | tf_op jit(solution)/shard_map/ppermute | solution.py:239
  534.6 65.7 %collective-permute-start.75 = (bf16[2,256,1024]{2,1,0:T(8,128)(2,1)}, bf16[2,256,1024]{2,1,0:T(8,128)(2,1)}, u32[]{:S(2)}, u32[]{:S(2)}) collective-permute-start(bf16[2,256,1024]{2,1,0:T(8,128)(2,1)} %fusion.21), channel_id=1, source_target_pairs={{16,0},{17,1},{18,2},{19,3},{20,4},{21,5},{22,6},{23,7},{24,8},{25... | collective-permute-start | bytes 3145736 | tf_op jit(solution)/shard_map/ppermute | solution.py:239
  546.9 15.6 %collective-permute-start.86 = (f32[16,768]{1,0:T(8,128)S(1)}, f32[16,768]{1,0:T(8,128)S(1)}, u32[]{:S(2)}, u32[]{:S(2)}) collective-permute-start(f32[16,768]{1,0:T(8,128)S(1)} %broadcast_select_fusion.20), channel_id=1, source_target_pairs={{0,16},{16,0},{1,17},{17,1},{2,18},{18,2},{3,19},{19,3},{4,20},{20... | collective-permute-start | bytes 147464 | tf_op jit(solution)/shard_map/ppermute | solution.py:16
  590.7 15.5 %collective-permute-start.71 = (bf16[2,256,256]{2,1,0:T(8,128)(2,1)S(1)}, bf16[2,256,256]{2,1,0:T(8,128)(2,1)S(1)}, u32[]{:S(2)}, u32[]{:S(2)}) collective-permute-start(bf16[2,256,256]{2,1,0:T(8,128)(2,1)S(1)} %copy-done.46), channel_id=1, source_target_pairs={{0,16},{1,17},{2,18},{3,19},{4,20},{5,21},{6,22},{7,23},{8,24},{9,... | collective-permute-start | bytes 786440 | tf_op jit(solution)/shard_map/ppermute | solution.py:239
  593.4 45.7 %collective-permute-start.65 = (bf16[2,256,768]{1,2,0:T(8,128)(2,1)}, bf16[2,256,768]{1,2,0:T(8,128)(2,1)}, u32[]{:S(2)}, u32[]{:S(2)}) collective-permute-start(bf16[2,256,768]{1,2,0:T(8,128)(2,1)} %fusion.38), channel_id=1, source_target_pairs={{0,16},{1,17},{2,18},{3,19},{4,20},{5,21},{6,22},{7,23},{8,24},{9,... | collective-permute-start | bytes 2359304 | tf_op jit(solution)/shard_map/ppermute | solution.py:239
  595.6 18.9 %collective-permute-start.62 = (bf16[2,256,768]{1,2,0:T(8,128)(2,1)}, bf16[2,256,768]{1,2,0:T(8,128)(2,1)S(1)}, u32[]{:S(2)}, u32[]{:S(2)}) collective-permute-start(bf16[2,256,768]{1,2,0:T(8,128)(2,1)} %bitcast.386), channel_id=1, source_target_pairs={{0,8},{4,12},{8,0},{12,4},{1,9},{5,13},{9,1},{13,5},{2,10},{6,14},... | collective-permute-start | bytes 2359304 | tf_op jit(solution)/shard_map/ppermute | solution.py:16
  606.1 32.8 %collective-permute-start.84 = (bf16[256,1024]{1,0:T(8,128)(2,1)}, bf16[256,1024]{1,0:T(8,128)(2,1)S(1)}, u32[]{:S(2)}, u32[]{:S(2)}) collective-permute-start(bf16[256,1024]{1,0:T(8,128)(2,1)} %dynamic-slice_bitcast_fusion.4), channel_id=1, source_target_pairs={{0,4},{4,0},{8,12},{12,8},{1,5},{5,1},{9,13},{13,9},{2,6},{6,2},{1... | collective-permute-start | bytes 1572872 | tf_op jit(solution)/shard_map/ppermute | solution.py:16
  610.9 38.5 %collective-permute-start.78 = (bf16[256,1024]{1,0:T(8,128)(2,1)}, bf16[256,1024]{1,0:T(8,128)(2,1)}, u32[]{:S(2)}, u32[]{:S(2)}) collective-permute-start(bf16[256,1024]{1,0:T(8,128)(2,1)} %dynamic-slice_bitcast_fusion.5), channel_id=1, source_target_pairs={{0,4},{4,0},{8,12},{12,8},{1,5},{5,1},{9,13},{13,9},{2,6},{6,2},{1... | collective-permute-start | bytes 1572872 | tf_op jit(solution)/shard_map/ppermute | solution.py:16
  624.4 22.6 %collective-permute-start.63 = (bf16[2,256,768]{1,2,0:T(8,128)(2,1)}, bf16[2,256,768]{1,2,0:T(8,128)(2,1)}, u32[]{:S(2)}, u32[]{:S(2)}) collective-permute-start(bf16[2,256,768]{1,2,0:T(8,128)(2,1)} %fusion.39), channel_id=1, source_target_pairs={{16,0},{17,1},{18,2},{19,3},{20,4},{21,5},{22,6},{23,7},{24,8},{25... | collective-permute-start | bytes 2359304 | tf_op jit(solution)/shard_map/ppermute | solution.py:239
  636.0 15.3 %collective-permute-start.61 = (bf16[2,64,1024]{2,1,0:T(8,128)(2,1)S(1)}, bf16[2,64,1024]{2,1,0:T(8,128)(2,1)S(1)}, u32[]{:S(2)}, u32[]{:S(2)}) collective-permute-start(bf16[2,64,1024]{2,1,0:T(8,128)(2,1)S(1)} %broadcast_select_fusion.13), channel_id=1, source_target_pairs={{0,16},{16,0},{1,17},{17,1},{2,18},{18,2},{3,19},{19,3},{4,20},{20... | collective-permute-start | bytes 786440 | tf_op jit(solution)/shard_map/ppermute | solution.py:16
  639.0 43.9 %collective-permute-start.85 = (bf16[256,1024]{1,0:T(8,128)(2,1)S(1)}, bf16[256,1024]{1,0:T(8,128)(2,1)S(1)}, u32[]{:S(2)}, u32[]{:S(2)}) collective-permute-start(bf16[256,1024]{1,0:T(8,128)(2,1)S(1)} %bitcast_select_fusion), channel_id=1, source_target_pairs={{0,2},{1,3},{2,0},{3,1},{4,6},{5,7},{6,4},{7,5},{8,10},{9,11},{10,... | collective-permute-start | bytes 1572872 | tf_op jit(solution)/shard_map/ppermute | solution.py:16
  651.3 42.9 %collective-permute-start.79 = (bf16[256,1024]{1,0:T(8,128)(2,1)}, bf16[256,1024]{1,0:T(8,128)(2,1)}, u32[]{:S(2)}, u32[]{:S(2)}) collective-permute-start(bf16[256,1024]{1,0:T(8,128)(2,1)} %bitcast_select_fusion.2), channel_id=1, source_target_pairs={{0,2},{1,3},{2,0},{3,1},{4,6},{5,7},{6,4},{7,5},{8,10},{9,11},{10,... | collective-permute-start | bytes 1572872 | tf_op jit(solution)/shard_map/ppermute | solution.py:16
  653.8 48.6 %collective-permute-start.67 = (bf16[256,768]{0,1:T(8,128)(2,1)}, bf16[256,768]{0,1:T(8,128)(2,1)S(1)}, u32[]{:S(2)}, u32[]{:S(2)}) collective-permute-start(bf16[256,768]{0,1:T(8,128)(2,1)} %bitcast_select_fusion.4), channel_id=1, source_target_pairs={{0,2},{1,3},{2,0},{3,1},{4,6},{5,7},{6,4},{7,5},{8,10},{9,11},{10,... | collective-permute-start | bytes 1179656 | tf_op jit(solution)/shard_map/ppermute | solution.py:16
  (184 other events, 1774.1 us)
